TPU v7x, 768 devices: a whole 4x8x12 slice. The times are simulated.
768 devices in a mesh: dp: 48 (over y_lo, z), weight: 16 (over x, y_hi, core).
Axes of the slice: x: 4, y: 8 (y_hi: 2, y_lo: 4; y = y_hi * 4 + y_lo), z: 12, core: 2. Of those that a mesh axis runs over, the one named last changes fastest.
Arguments:
- tokens: bfloat16 [6144, 8192], P('dp'), may hold values from -6 to 6
- block_values: bfloat16 [16, 48, 128, 128], P('weight', 'dp'), may hold values from -0.4375 to 0.4375
- block_rows: int32 [16, 48], P('weight'), may hold values from 0 to 63, as said below
- block_cols: int32 [16, 48], P('weight'), may hold values from 0 to 15
- block_counts: int32 [16], P('weight'), may hold values from 1 to 48, as said below
- cotangent: bfloat16 [6144, 32768], P('dp', 'weight'), may hold values from -6 to 6
Outputs:
- activated: bfloat16 [6144, 32768], P('dp', 'weight')
- input_grad: bfloat16 [6144, 8192], P('dp', 'weight')
- block_grad: float32 [16, 48, 128, 128], P('weight', 'dp')
Inputs may be any that keep to these rules, and one draw needn't show every extreme that they name: In each panel the 48 pairs (block_rows, block_cols) name distinct blocks. `block_counts`: some panel has all 48 slots live.
All inputs are finite; a program needn't handle non-finite values.
Results may differ from a plain program's by a relative error of at most 0.015.
Values may be sent and summed in bfloat16 or wider, within the bound.
A program may use at most 64 MiB of HBM per device.

v0:
```python
import math

import jax
import jax.numpy as jnp
from jax import lax
from jax.sharding import PartitionSpec as P


def local(tokens, block_values, block_rows, block_cols, block_counts, cotangent):
    tok_count = tokens.shape[0]
    feat_width = tokens.shape[1]
    panel_width = cotangent.shape[1]
    col_blocks = panel_width // 128
    row_blocks = feat_width // 128
    slot_rows = block_rows[0]
    slot_cols = block_cols[0]
    slot_count = slot_rows.shape[0]
    live_mask = jnp.arange(slot_count) < block_counts[0]
    live_slots = live_mask.astype(jnp.float32)
    col_ids = jnp.where(live_mask, slot_cols, col_blocks)
    row_ids = jnp.where(live_mask, slot_rows, row_blocks)
    blocked = tokens.reshape(tok_count, row_blocks, 128)
    picked = jnp.take(blocked, slot_rows, axis=1)
    owned = block_values[0]
    gathered = lax.all_gather(owned, "dp", axis=0, tiled=True)
    contrib = jnp.einsum("tsk,skn->stn", picked, gathered, preferred_element_type=jnp.float32)
    summed = jax.ops.segment_sum(contrib, col_ids, num_segments=col_blocks)
    preact = jnp.transpose(summed, (1, 0, 2)).reshape(tok_count, panel_width)
    gate_sig = jax.nn.sigmoid(preact)
    activated = (preact * gate_sig).astype(jnp.bfloat16)
    grad_pre = (
        cotangent.astype(jnp.float32) * gate_sig * (1.0 + preact * (1.0 - gate_sig))
    ).astype(jnp.bfloat16)
    grad_slot = jnp.take(grad_pre.reshape(tok_count, col_blocks, 128), slot_cols, axis=1)
    grad_scale = 1.0 / math.sqrt(tok_count * lax.axis_size("dp"))
    partial_value = jnp.einsum(
        "tsk,tsn->skn", picked, grad_slot, preferred_element_type=jnp.float32
    )
    partial_value = partial_value * (live_slots * grad_scale)[:, None, None]
    block_grad = lax.psum_scatter(partial_value, "dp", scatter_dimension=0, tiled=True).reshape(
        block_values.shape
    )
    back_terms = jnp.einsum("tsn,skn->stk", grad_slot, gathered, preferred_element_type=jnp.float32)
    spread_back = jax.ops.segment_sum(back_terms, row_ids, num_segments=row_blocks).astype(
        jnp.bfloat16
    )
    spread_back = jnp.transpose(spread_back, (1, 0, 2)).reshape(tok_count, feat_width)
    input_grad = lax.psum_scatter(
        spread_back.astype(jnp.float32).astype(jnp.bfloat16),
        "weight",
        scatter_dimension=1,
        tiled=True,
    )
    return (activated, input_grad, block_grad)


def solution(mesh):
    placed = (
        P("dp", None),
        P("weight", "dp", None, None),
        P("weight", None),
        P("weight", None),
        P("weight"),
        P("dp", "weight"),
    )
    return jax.shard_map(
        local,
        mesh=mesh,
        in_specs=placed,
        out_specs=(P("dp", "weight"), P("dp", "weight"), P("weight", "dp", None, None)),
        check_vma=False,
    )
```

profile of v0, /device:TPU:6, one launch (start us, length us, event | category | flops | bytes accessed | tf_op | source)
XLA Modules:
  0.0 632.1 jit_solution(6808482974866729688)
XLA Ops:
  7.2 0.0 all-gather.3.cloned.1.call-start
  7.2 0.7 all-gather.3.cloned.1.call-update
  7.9 0.0 reduce-scatter.3.cloned.1.call-start
  8.6 1.3 copy.28
  9.9 3.2 copy.25
  13.1 0.0 copy-start.1
  13.2 0.0 copy-start.2
  13.2 2.9 copy.26
  16.1 0.0 copy-done.1
  16.1 0.0 copy-done.2
  16.1 2.4 gather_fusion
  18.6 225.6 %all-gather.3.cloned.1.call-done = bf16[48,1,128,128]{3,2,1,0:T(8,128)(2,1)} async-done(((bf16[1,1,128,128]{3,2,1,0:T(8,128)(2,1)}), bf16[48,1,128,128]{3,2,1,0:T(8,128)(2,1)}) %all-gather.3.cloned.1.call-update) | async-done | bytes 1572880 | tf_op jit(solution)/shard_map/all_gather | solution.py:25
  244.2 3.7 fusion.4
  247.9 0.1 broadcast_in_dim.34
  248.0 6.7 %scatter_fusion = f32[16,128,128]{2,1,0:T(8,128)S(1)} fusion(f32[16,128,128]{2,1,0:T(8,128)S(1)} %broadcast_in_dim.34, s32[48]{0:T(128)S(1)} %get-tuple-element.15, f32[48,128,128]{2,1,0:T(8,128)} %fusion.4), kind=kCustom, calls=%fused_computation.2 | custom fusion | flops 786432 | bytes 9437376 | tf_op jit(solution)/shard_map/scatter-add | solution.py:27
  254.7 1.3 copy.27
  256.0 2.5 fusion.14
  258.5 1.0 copy.29
  259.5 1.9 gather_fusion.1
  261.4 4.3 fusion.1
  265.7 2.5 broadcast_in_dim.38
  268.2 9.9 %scatter_fusion.1 = f32[64,128,128]{2,1,0:T(8,128)} fusion(f32[64,128,128]{2,1,0:T(8,128)} %broadcast_in_dim.38, s32[48]{0:T(128)S(1)} %get-tuple-element.13, f32[48,128,128]{2,1,0:T(8,128)} %fusion.1), kind=kCustom, calls=%fused_computation.3 | custom fusion | flops 786432 | bytes 9437376 | tf_op jit(solution)/shard_map/scatter-add | solution.py:44
  278.1 3.9 convert_bitcast_fusion
  281.9 4.1 copy.30
  286.0 0.0 reduce-scatter.3.cloned.1.call-update
  286.0 0.0 reduce-scatter.5.cloned.1.call-start
  286.1 2.6 convolution_multiply_fusion
  288.7 0.0 copy-start
  288.7 0.0 reduce-scatter.5.cloned.1.call-update
  288.7 1.0 copy-done
  289.7 1.0 copy.32
  290.7 89.9 %reduce-scatter.3.cloned.1.call-done = bf16[128,512]{0,1:T(8,128)(2,1)} async-done(((bf16[128,8192]{0,1:T(8,128)(2,1)}), bf16[128,512]{0,1:T(8,128)(2,1)}) %reduce-scatter.3.cloned.1.call-update) | async-done | bytes 131088 | tf_op jit(solution)/shard_map/reduce_scatter | solution.py:48
  380.6 1.7 copy.33
  382.3 243.2 %reduce-scatter.5.cloned.1.call-done = f32[1,128,128]{2,1,0:T(8,128)} async-done(((f32[48,128,128]{2,1,0:T(8,128)}), f32[1,128,128]{2,1,0:T(8,128)}) %reduce-scatter.5.cloned.1.call-update) | async-done | bytes 65552 | tf_op jit(solution)/shard_map/reduce_scatter | solution.py:40
  (5 shorter events, 0.0 us)
Async XLA Ops:
  7.2 237.0 %all-gather.3.cloned.1.call-start = ((), (), s32[]{:S(2)}) async-start(), calls=%async_computation.4 | async-start | bytes 1605632 | tf_op jit(solution)/shard_map/all_gather | solution.py:25
  7.9 372.8 %reduce-scatter.3.cloned.1.call-start = ((), (), s32[]{:S(2)}) async-start(), calls=%async_computation.2 | async-start | bytes 2228224 | tf_op jit(solution)/shard_map/reduce_scatter | solution.py:48
  13.1 2.9 copy-start.1
  13.2 2.9 copy-start.2
  286.0 339.5 %reduce-scatter.5.cloned.1.call-start = ((), (), s32[]{:S(2)}) async-start(), calls=%async_computation.3 | async-start | bytes 3211264 | tf_op jit(solution)/shard_map/reduce_scatter | solution.py:40
  288.7 1.0 copy-start
Sparse Core Ops, SparseCore 0:
  10.4 233.7 all-gather.2
  286.2 94.4 reduce-scatter.2
  384.3 241.1 reduce-scatter.4
where the time goes:
time: 634 us; the launch traced here: 632 us
  waiting for transfers between devices  559 us (88%)
  local copies, waits for them, and re-layouts  24.4 us (4%)
  other arithmetic  23 us (4%)
  between operations  14.5 us (2%)
  matrix products  10.6 us (2%)
    reduce_scatter x1, waiting for transfers between devices, local(): lax.psum_scatter(partial_value, 'dp', scatter_dimension=0, tiled=True)  243 us
    all_gather x1, waiting for transfers between devices, local(): gathered = lax.all_gather(owned, 'dp', axis=0, tiled=True)  226 us
    reduce_scatter x1, waiting for transfers between devices, local(): lax.psum_scatter(spread_back.astype(jnp.float32).astype(jnp.bfloat16), 'w...  89.9 us
  transfers between devices with their start and end apart: 3, of which 3 were waited for; matrix products, arithmetic and copies ran while one was open for 2% of the time, Pallas kernels for 0%

commit v1 on v0

v1 whole, which is shorter than its diff:
```python
import functools
import math

import jax
import jax.numpy as jnp
from jax import lax
from jax.experimental import pallas as pl
from jax.experimental.pallas import tpu as pltpu
from jax.sharding import PartitionSpec as P

MESH = pl.DeviceIdType.MESH
NY, NZ, NX = 4, 12, 4
F32, BF16 = jnp.float32, jnp.bfloat16


def mod(a, n):
    return lax.rem(a + n, n)


def hops(delta, side):
    long_way, short_way = NZ // 2, NZ - 1 - NZ // 2
    return long_way if (delta + side) % 2 == 0 else short_way


def greet(partners):
    barrier = pltpu.get_barrier_semaphore()
    for dp, weight in partners:
        pl.semaphore_signal(barrier, inc=1, device_id=(dp, weight), device_id_type=MESH)
    pl.semaphore_wait(barrier, len(partners))


def gather_kernel(own_ref, out_ref, own_sem, y_send, y_recv, z_send, z_recv):
    dp, weight = lax.axis_index("dp"), lax.axis_index("weight")
    j, z = dp // NZ, lax.rem(dp, NZ)
    sides = (mod(z + 1, NZ), mod(z - 1, NZ))
    greet(
        [(mod(j + delta, NY) * NZ + z, weight) for delta in range(1, NY)]
        + [(j * NZ + side, weight) for side in sides]
    )
    keep = pltpu.make_async_copy(own_ref, out_ref.at[dp], own_sem)
    keep.start()

    def y_copy(delta):
        return pltpu.make_async_remote_copy(
            src_ref=own_ref,
            dst_ref=out_ref.at[dp],
            send_sem=y_send.at[delta - 1],
            recv_sem=y_recv.at[delta - 1],
            device_id=(mod(j + delta, NY) * NZ + z, weight),
            device_id_type=MESH,
        )

    def z_copy(side, delta, step):
        back = -step if side == 0 else step
        slot = mod(j - delta, NY) * NZ + mod(z + back, NZ)
        return pltpu.make_async_remote_copy(
            src_ref=own_ref if (delta == 0 and step == 0) else out_ref.at[slot],
            dst_ref=out_ref.at[slot],
            send_sem=z_send.at[side, delta, step],
            recv_sem=z_recv.at[side, delta, step],
            device_id=(j * NZ + sides[side], weight),
            device_id_type=MESH,
        )

    started = []
    for side in range(2):
        copy = z_copy(side, 0, 0)
        copy.start()
        started.append(copy)
    for delta in range(1, NY):
        copy = y_copy(delta)
        copy.start()
        started.append(copy)
    for delta in range(1, NY):
        y_copy(delta).wait_recv()
        for side in range(2):
            copy = z_copy(side, delta, 0)
            copy.start()
            started.append(copy)
    for step in range(1, NZ // 2 + 1):
        for delta in range(NY):
            for side in range(2):
                if step > hops(delta, side):
                    continue
                z_copy(side, delta, step - 1).wait_recv()
                if step < hops(delta, side):
                    copy = z_copy(side, delta, step)
                    copy.start()
                    started.append(copy)
    for copy in started:
        copy.wait_send()
    keep.wait()


def gather_blocks(own, slots):
    size = own.shape
    return pl.pallas_call(
        gather_kernel,
        out_shape=jax.ShapeDtypeStruct((slots,) + size, own.dtype),
        in_specs=[pl.BlockSpec(memory_space=pltpu.VMEM)],
        out_specs=pl.BlockSpec(memory_space=pltpu.VMEM),
        scratch_shapes=[
            pltpu.SemaphoreType.DMA,
            pltpu.SemaphoreType.DMA((NY - 1,)),
            pltpu.SemaphoreType.DMA((NY - 1,)),
            pltpu.SemaphoreType.DMA((2, NY, NZ // 2)),
            pltpu.SemaphoreType.DMA((2, NY, NZ // 2)),
        ],
        compiler_params=pltpu.CompilerParams(collective_id=0, has_side_effects=True),
        name="gather_blocks",
    )(own)


UNROLL = 8


def local_kernel(
    rows_ref, cols_ref, count_ref, tokens_ref, blocks_ref, cot_ref,
    act_ref, back_ref, grads_ref, acc_ref, grad_pre_ref, back_acc_ref,
):
    slots = blocks_ref.shape[0]
    col_blocks = grad_pre_ref.shape[0]
    row_blocks = back_acc_ref.shape[0] - 1
    count = count_ref[0]
    acc_ref[...] = jnp.zeros_like(acc_ref)

    def picked(slot):
        return tokens_ref[:, pl.ds(pl.multiple_of(rows_ref[slot] * 128, 128), 128)]

    def forward(group, carry):
        for at in range(UNROLL):
            slot = group * UNROLL + at
            col = jnp.where(slot < count, cols_ref[slot], col_blocks)
            acc_ref[col] += jnp.dot(picked(slot), blocks_ref[slot], preferred_element_type=F32)
        return carry

    lax.fori_loop(0, slots // UNROLL, forward, 0)
    back_acc_ref[...] = jnp.zeros_like(back_acc_ref)
    for col in range(col_blocks):
        here = slice(col * 128, col * 128 + 128)
        preact = acc_ref[col]
        gate = jax.nn.sigmoid(preact)
        act_ref[:, here] = (preact * gate).astype(BF16)
        grad_pre_ref[col] = (
            cot_ref[:, here].astype(F32) * gate * (1.0 + preact * (1.0 - gate))
        ).astype(BF16)

    def backward(group, carry):
        for at in range(UNROLL):
            slot = group * UNROLL + at
            live = slot < count
            row = jnp.where(live, rows_ref[slot], row_blocks)
            grad = grad_pre_ref[cols_ref[slot]]
            back_acc_ref[row] += lax.dot_general(
                grad, blocks_ref[slot], (((1,), (1,)), ((), ())), preferred_element_type=F32
            )
            partial = lax.dot_general(
                picked(slot), grad, (((0,), (0,)), ((), ())), preferred_element_type=F32
            )
            grads_ref[slot] = (partial * live.astype(F32)).astype(BF16)
        return carry

    lax.fori_loop(0, slots // UNROLL, backward, 0)
    wide = back_ref.shape[2] // 128
    for row in range(row_blocks):
        at = (row % wide) * 128
        back_ref[row // wide, :, at:at + 128] = back_acc_ref[row].astype(BF16)


def local_work(rows, cols, count, tokens, blocks, cot, owners):
    tok, feat = tokens.shape
    slots = blocks.shape[0]
    panel = cot.shape[1]
    smem = pl.BlockSpec(memory_space=pltpu.SMEM)
    vmem = pl.BlockSpec(memory_space=pltpu.VMEM)
    return pl.pallas_call(
        local_kernel,
        out_shape=(
            jax.ShapeDtypeStruct((tok, panel), BF16),
            jax.ShapeDtypeStruct((owners, tok, feat // owners), BF16),
            jax.ShapeDtypeStruct((slots, 128, 128), BF16),
        ),
        in_specs=[smem, smem, smem, vmem, vmem, vmem],
        out_specs=(vmem, vmem, vmem),
        scratch_shapes=[
            pltpu.VMEM((panel // 128 + 1, tok, 128), F32),
            pltpu.VMEM((panel // 128, tok, 128), BF16),
            pltpu.VMEM((feat // 128 + 1, tok, 128), F32),
        ],
        compiler_params=pltpu.CompilerParams(vmem_limit_bytes=32 << 20),
        name="local_work",
    )(rows, cols, count, tokens, blocks, cot)


def reduce_kernel(
    scale, back_ref, grads_ref, in_grad_ref, block_grad_ref,
    z_buf, y_buf, y_out, c_buf, x_sum, x_buf, h_out, h_buf,
    z_send, z_recv, y_send, y_recv, c_send, c_recv, x_send, x_recv, h_send, h_recv,
):
    dp, weight = lax.axis_index("dp"), lax.axis_index("weight")
    j, z = dp // NZ, lax.rem(dp, NZ)
    x, h, core = weight // 4, lax.rem(weight // 2, 2), lax.rem(weight, 2)
    sides = (mod(z + 1, NZ), mod(z - 1, NZ))
    x_sides = (mod(x + 1, NX), mod(x - 1, NX))
    sibling = weight + 1 - 2 * core
    x_weight = [(side * 2 + h) * 2 + core for side in x_sides]
    h_weight = (x * 2 + 1 - h) * 2 + core
    greet(
        [(mod(j + delta, NY) * NZ + z, weight) for delta in range(1, NY)]
        + [(j * NZ + side, weight) for side in sides]
        + [(dp, sibling)]
        + [(dp, side) for side in x_weight]
        + [(dp, h_weight)]
    )
    started = []

    def go(copy):
        copy.start()
        started.append(copy)

    def send(src, dst, send_sem, recv_sem, device):
        return pltpu.make_async_remote_copy(
            src_ref=src, dst_ref=dst, send_sem=send_sem, recv_sem=recv_sem,
            device_id=device, device_id_type=MESH,
        )

    def z_slot(side, delta, step):
        ahead = hops(delta, side) - step
        return mod(j + delta, NY) * NZ + mod(z + (ahead if side == 0 else -ahead), NZ)

    def z_copy(side, delta, step):
        src = grads_ref.at[z_slot(side, delta, 0)] if step == 0 else z_buf.at[side, delta, step - 1]
        return send(
            src, z_buf.at[side, delta, step], z_send.at[side, delta, step],
            z_recv.at[side, delta, step], (j * NZ + sides[side], weight),
        )

    def z_step(step):
        for delta in range(NY):
            for side in range(2):
                if step >= hops(delta, side):
                    continue
                if step > 0:
                    z_copy(side, delta, step - 1).wait_recv()
                    z_buf[side, delta, step - 1] = (
                        z_buf[side, delta, step - 1].astype(F32)
                        + grads_ref[z_slot(side, delta, step)].astype(F32)
                    ).astype(BF16)
                go(z_copy(side, delta, step))

    def owner(dx, half, which):
        return (mod(x + dx, NX) * 2 + mod(h + half, 2)) * 2 + which

    def c_copy(dx, half):
        return send(
            back_ref.at[owner(dx, half, 1 - core)], c_buf.at[dx, half],
            c_send.at[dx, half], c_recv.at[dx, half], (dp, sibling),
        )

    def c_sum(dx, half):
        c_copy(dx, half).wait_recv()
        return c_buf[dx, half].astype(F32) + back_ref[owner(dx, half, core)].astype(F32)

    def x_copy(side, what):
        return send(
            x_sum.at[side, what], x_buf.at[side, what], x_send.at[side, what],
            x_recv.at[side, what], (dp, x_weight[side]),
        )

    def h_copy():
        return send(h_out, h_buf, h_send, h_recv, (dp, h_weight))

    order = [(2, 1), (2, 0), (3, 1), (1, 0), (1, 1), (3, 0), (0, 1), (0, 0)]
    for dx, half in order[:2]:
        go(c_copy(dx, half))
    z_step(0)
    for dx, half in order[2:]:
        go(c_copy(dx, half))
    for half, side in ((1, 0), (0, 1)):
        x_sum[side, 0] = c_sum(2, half).astype(BF16)
        go(x_copy(side, 0))
    for half, side, dx in ((1, 1, 3), (0, 0, 1)):
        x_sum[side, 1] = c_sum(dx, half).astype(BF16)
        go(x_copy(side, 1))
    z_step(1)
    for half, side, dx in ((1, 0, 1), (0, 1, 3)):
        own = c_sum(dx, half)
        x_copy(side, 0).wait_recv()
        x_sum[side, 2] = (own + x_buf[side, 0].astype(F32)).astype(BF16)
        go(x_copy(side, 2))
    z_step(2)
    total = c_sum(0, 1)
    x_copy(1, 1).wait_recv()
    total += x_buf[1, 1].astype(F32)
    z_step(3)
    x_copy(0, 2).wait_recv()
    h_out[...] = (total + x_buf[0, 2].astype(F32)).astype(BF16)
    go(h_copy())
    z_step(4)
    total = c_sum(0, 0)
    x_copy(0, 1).wait_recv()
    total += x_buf[0, 1].astype(F32)
    x_copy(1, 2).wait_recv()
    total += x_buf[1, 2].astype(F32)
    z_step(5)

    def z_total(delta):
        value = grads_ref[mod(j + delta, NY) * NZ + z].astype(F32)
        for side in range(2):
            last = hops(delta, side) - 1
            z_copy(side, delta, last).wait_recv()
            value += z_buf[side, delta, last].astype(F32)
        return value

    def y_copy(delta):
        return send(
            y_out.at[delta - 1], y_buf.at[delta - 1], y_send.at[delta - 1], y_recv.at[delta - 1],
            (mod(j + delta, NY) * NZ + z, weight),
        )

    for delta in (2, 1, 3):
        y_out[delta - 1] = z_total(delta).astype(BF16)
        go(y_copy(delta))
    grad = z_total(0)
    h_copy().wait_recv()
    in_grad_ref[...] = (total + h_buf[...].astype(F32)).astype(BF16)
    for delta in (2, 1, 3):
        y_copy(delta).wait_recv()
        grad += y_buf[delta - 1].astype(F32)
    block_grad_ref[...] = grad * scale
    for copy in started:
        copy.wait_send()


def reduce_all(back, grads, scale):
    owners, tok, width = back.shape
    vmem = pl.BlockSpec(memory_space=pltpu.VMEM)
    part = (tok, width)
    dma = pltpu.SemaphoreType.DMA
    return pl.pallas_call(
        functools.partial(reduce_kernel, scale),
        out_shape=(
            jax.ShapeDtypeStruct(part, BF16),
            jax.ShapeDtypeStruct(grads.shape[1:], F32),
        ),
        in_specs=[vmem, vmem],
        out_specs=(vmem, vmem),
        scratch_shapes=[
            pltpu.VMEM((2, NY, NZ // 2) + grads.shape[1:], BF16),
            pltpu.VMEM((NY - 1,) + grads.shape[1:], BF16),
            pltpu.VMEM((NY - 1,) + grads.shape[1:], BF16),
            pltpu.VMEM((NX, 2) + part, BF16),
            pltpu.VMEM((2, 3) + part, BF16),
            pltpu.VMEM((2, 3) + part, BF16),
            pltpu.VMEM(part, BF16),
            pltpu.VMEM(part, BF16),
            dma((2, NY, NZ // 2)),
            dma((2, NY, NZ // 2)),
            dma((NY - 1,)),
            dma((NY - 1,)),
            dma((NX, 2)),
            dma((NX, 2)),
            dma((2, 3)),
            dma((2, 3)),
            dma,
            dma,
        ],
        compiler_params=pltpu.CompilerParams(
            collective_id=1, has_side_effects=True, vmem_limit_bytes=32 << 20
        ),
        name="reduce_all",
    )(back, grads)


def local(tokens, block_values, block_rows, block_cols, block_counts, cotangent):
    owners = lax.axis_size("weight")
    blocks = gather_blocks(block_values[0, 0], block_rows.shape[1])
    activated, back, grads = local_work(
        block_rows[0], block_cols[0], block_counts, tokens, blocks, cotangent, owners
    )
    scale = 1.0 / math.sqrt(tokens.shape[0] * lax.axis_size("dp"))
    input_grad, block_grad = reduce_all(back, grads, scale)
    return (activated, input_grad, block_grad.reshape(block_values.shape))


def solution(mesh):
    placed = (
        P("dp", None),
        P("weight", "dp", None, None),
        P("weight", None),
        P("weight", None),
        P("weight"),
        P("dp", "weight"),
    )
    return jax.shard_map(
        local,
        mesh=mesh,
        in_specs=placed,
        out_specs=(P("dp", "weight"), P("dp", "weight"), P("weight", "dp", None, None)),
        check_vma=False,
    )
```

time: 634 us -> 88.8 us (0.14)
  waiting for transfers between devices: 559 us -> 0 us
  Pallas kernels: 0 us -> 80.1 us
  other arithmetic: 23 us -> 0 us
  local copies, waits for them, and re-layouts: 24.4 us -> 6.63 us
  between operations: 14.5 us -> 1.31 us
  matrix products: 10.6 us -> 0 us
    reduce_scatter x2 -> x0, waiting for transfers between devices: 333 us -> none  [the longest x1 243 us: local(): lax.psum_scatter(partial_value, 'dp', scatter_dimension=0, tiled=True)]
    all_gather x1 -> x0, waiting for transfers between devices: 226 us -> none  [local(): gathered = lax.all_gather(owned, 'dp', axis=0, tiled=True)]
    pallas_call x0 -> x3, Pallas kernels: none -> 80.1 us  [the longest x1 42.1 us: gather_blocks(): pl.pallas_call(gather_kernel, out_shape=jax.ShapeDtypeStruct((slots,) + s...]
    scatter-add x2 -> x0, other arithmetic: 16.6 us -> none  [the longest x1 9.86 us: local(): jax.ops.segment_sum(back_terms, row_ids, num_segments=row_blocks)]
    dot_general x3 -> x0, matrix products: 10.6 us -> none  [the longest x1 4.33 us: local(): jnp.einsum('tsn,skn->stk', grad_slot, gathered, preferred_element_type=jn...]
  transfers between devices with their start and end apart: 3 -> 0, of which waited for: 3 -> 0; matrix products, arithmetic and copies ran while one was open for 2% -> 0% of each run, Pallas kernels for 0% -> 0%
where the time goes in v1:
time: 88.8 us; the launch traced here: 88.1 us
  Pallas kernels  80.1 us (90%)
  local copies, waits for them, and re-layouts  6.63 us (7%)
  between operations  1.31 us (1%)
    pallas_call x1, Pallas kernels, gather_blocks(): pl.pallas_call(gather_kernel, out_shape=jax.ShapeDtypeStruct((slots,) + s...  42.1 us
    pallas_call x1, Pallas kernels, reduce_all(): pl.pallas_call(functools.partial(reduce_kernel, scale), out_shape=(jax.Sh...  32.1 us
    unnamed x12, local copies, waits for them, and re-layouts  6.63 us
    pallas_call x1, Pallas kernels, local_work(): pl.pallas_call(local_kernel, out_shape=(jax.ShapeDtypeStruct((tok, panel)...  6.03 us

profile of v1, /device:TPU:6, one launch (start us, length us, event | category | flops | bytes accessed | tf_op | source)
XLA Modules:
  0.0 88.1 jit_solution(15944992236734205505)
XLA Ops:
  1.3 42.1 %gather_blocks.1.blocks_ref = bf16[48,128,128]{2,1,0:T(8,128)(2,1)} custom-call(bf16[128,128]{1,0:T(8,128)(2,1)} %bitcast.7), custom_call_target="tpu_custom_call" | custom-call | tf_op jit(solution)/shard_map/gather_blocks/pallas_call | solution.py:97
  43.3 0.0 copy-start
  43.4 1.4 %copy-done = bf16[48,128,128]{2,1,0:T(8,128)(2,1)S(1)} copy-done((bf16[48,128,128]{2,1,0:T(8,128)(2,1)S(1)}, bf16[48,128,128]{2,1,0:T(8,128)(2,1)}, u32[]{:S(2)}) %copy-start) | copy-done | bytes 1572888
  44.8 0.0 copy-start.1
  44.8 1.6 %copy-done.1 = bf16[128,8192]{1,0:T(8,128)(2,1)S(1)} copy-done((bf16[128,8192]{1,0:T(8,128)(2,1)S(1)}, bf16[128,8192]{1,0:T(8,128)(2,1)}, u32[]{:S(2)}) %copy-start.1) | copy-done | bytes 2097176
  46.3 0.0 copy-start.2
  46.4 1.0 %copy-done.2 = bf16[128,2048]{1,0:T(8,128)(2,1)S(1)} copy-done((bf16[128,2048]{1,0:T(8,128)(2,1)S(1)}, bf16[128,2048]{1,0:T(8,128)(2,1)}, u32[]{:S(2)}) %copy-start.2) | copy-done | bytes 524312
  47.4 0.0 copy-start.3
  47.4 0.7 copy-done.3
  48.0 0.0 copy-start.4
  48.0 0.7 copy-done.4
  48.7 6.0 %local_work.1 = (bf16[128,2048]{1,0:T(8,128)(2,1)}, bf16[16,128,512]{2,1,0:T(8,128)(2,1)S(1)}, bf16[48,128,128]{2,1,0:T(8,128)(2,1)S(1)}) custom-call(s32[48]{0:T(128)S(1)} %bitcast.5, s32[48]{0:T(128)S(1)} %bitcast.6, s32[1]{0:T(128)S(6)} %copy.11.count_ref, bf16[128,8192]{1,0:T(8,128)(2,1)S(1)} %copy-done.1, bf16[48,128,128]{2,1,0:T(8,128)(2,1)S(1)} %copy-done, ...), custom_call_target="tpu_custom_call" | custom-call | tf_op jit(solution)/shard_map/local_work/pallas_call | solution.py:176
  54.7 32.1 %reduce_all.1 = (bf16[128,512]{1,0:T(8,128)(2,1)S(1)}, f32[128,128]{1,0:T(8,128)S(1)}) custom-call(bf16[16,128,512]{2,1,0:T(8,128)(2,1)S(1)} %get-tuple-element.9.back_ref, bf16[48,128,128]{2,1,0:T(8,128)(2,1)S(1)} %get-tuple-element.10.grads_ref), custom_call_target="tpu_custom_call" | custom-call | tf_op jit(solution)/shard_map/reduce_all/pallas_call | solution.py:340
  86.8 0.7 copy.12
  87.4 0.6 copy.13
Async XLA Ops:
  43.3 1.4 %copy-start = (bf16[48,128,128]{2,1,0:T(8,128)(2,1)S(1)}, bf16[48,128,128]{2,1,0:T(8,128)(2,1)}, u32[]{:S(2)}) copy-start(bf16[48,128,128]{2,1,0:T(8,128)(2,1)} %gather_blocks.1.blocks_ref) | copy-start | bytes 4718596
  44.8 1.6 %copy-start.1 = (bf16[128,8192]{1,0:T(8,128)(2,1)S(1)}, bf16[128,8192]{1,0:T(8,128)(2,1)}, u32[]{:S(2)}) copy-start(bf16[128,8192]{1,0:T(8,128)(2,1)} %tokens_ref.1) | copy-start | bytes 6291460
  46.3 1.0 %copy-start.2 = (bf16[128,2048]{1,0:T(8,128)(2,1)S(1)}, bf16[128,2048]{1,0:T(8,128)(2,1)}, u32[]{:S(2)}) copy-start(bf16[128,2048]{1,0:T(8,128)(2,1)} %cot_ref.1) | copy-start | bytes 1572868
  47.4 0.7 copy-start.3
  48.0 0.7 copy-start.4

commit v2 on v1

--- a/solution.py
+++ b/solution.py
@@ -26,19 +26,24 @@
     barrier = pltpu.get_barrier_semaphore()
     for dp, weight in partners:
         pl.semaphore_signal(barrier, inc=1, device_id=(dp, weight), device_id_type=MESH)
-    pl.semaphore_wait(barrier, len(partners))
+
+    def wait():
+        pl.semaphore_wait(barrier, len(partners))
+
+    return wait
 
 
 def gather_kernel(own_ref, out_ref, own_sem, y_send, y_recv, z_send, z_recv):
     dp, weight = lax.axis_index("dp"), lax.axis_index("weight")
     j, z = dp // NZ, lax.rem(dp, NZ)
     sides = (mod(z + 1, NZ), mod(z - 1, NZ))
-    greet(
+    ready = greet(
         [(mod(j + delta, NY) * NZ + z, weight) for delta in range(1, NY)]
         + [(j * NZ + side, weight) for side in sides]
     )
     keep = pltpu.make_async_copy(own_ref, out_ref.at[dp], own_sem)
     keep.start()
+    ready()
 
     def y_copy(delta):
         return pltpu.make_async_remote_copy(
@@ -63,30 +68,29 @@
         )
 
     started = []
-    for side in range(2):
-        copy = z_copy(side, 0, 0)
+
+    def go(copy):
         copy.start()
         started.append(copy)
+
+    def z_step(delta, step):
+        for side in range(2):
+            if step > hops(delta, side):
+                continue
+            if step > 0:
+                z_copy(side, delta, step - 1).wait_recv()
+            if step < hops(delta, side):
+                go(z_copy(side, delta, step))
+
+    z_step(0, 0)
     for delta in range(1, NY):
-        copy = y_copy(delta)
-        copy.start()
-        started.append(copy)
-    for delta in range(1, NY):
-        y_copy(delta).wait_recv()
-        for side in range(2):
-            copy = z_copy(side, delta, 0)
-            copy.start()
-            started.append(copy)
-    for step in range(1, NZ // 2 + 1):
-        for delta in range(NY):
-            for side in range(2):
-                if step > hops(delta, side):
-                    continue
-                z_copy(side, delta, step - 1).wait_recv()
-                if step < hops(delta, side):
-                    copy = z_copy(side, delta, step)
-                    copy.start()
-                    started.append(copy)
+        go(y_copy(delta))
+    for step in range(NZ // 2 + 1):
+        z_step(0, step + 1)
+        for delta in (1, 3, 2):
+            if step == 0:
+                y_copy(delta).wait_recv()
+            z_step(delta, step)
     for copy in started:
         copy.wait_send()
     keep.wait()
@@ -94,11 +98,12 @@
 
 def gather_blocks(own, slots):
     size = own.shape
+    vmem = pl.BlockSpec(memory_space=pltpu.VMEM)
     return pl.pallas_call(
         gather_kernel,
         out_shape=jax.ShapeDtypeStruct((slots,) + size, own.dtype),
-        in_specs=[pl.BlockSpec(memory_space=pltpu.VMEM)],
-        out_specs=pl.BlockSpec(memory_space=pltpu.VMEM),
+        in_specs=[vmem],
+        out_specs=vmem,
         scratch_shapes=[
             pltpu.SemaphoreType.DMA,
             pltpu.SemaphoreType.DMA((NY - 1,)),
@@ -106,7 +111,10 @@
             pltpu.SemaphoreType.DMA((2, NY, NZ // 2)),
             pltpu.SemaphoreType.DMA((2, NY, NZ // 2)),
         ],
-        compiler_params=pltpu.CompilerParams(collective_id=0, has_side_effects=True),
+        compiler_params=pltpu.CompilerParams(
+            collective_id=0, has_side_effects=True, vmem_limit_bytes=4 << 20
+        ),
+        cost_estimate=pl.CostEstimate(flops=40_000_000_000, bytes_accessed=60_000_000, transcendentals=0),
         name="gather_blocks",
     )(own)
 
@@ -116,7 +124,7 @@
 
 def local_kernel(
     rows_ref, cols_ref, count_ref, tokens_ref, blocks_ref, cot_ref,
-    act_ref, back_ref, grads_ref, acc_ref, grad_pre_ref, back_acc_ref,
+    act_ref, back_ref, picked_ref, spread_ref, acc_ref, grad_pre_ref, back_acc_ref,
 ):
     slots = blocks_ref.shape[0]
     col_blocks = grad_pre_ref.shape[0]
@@ -124,14 +132,14 @@
     count = count_ref[0]
     acc_ref[...] = jnp.zeros_like(acc_ref)
 
-    def picked(slot):
-        return tokens_ref[:, pl.ds(pl.multiple_of(rows_ref[slot] * 128, 128), 128)]
-
     def forward(group, carry):
         for at in range(UNROLL):
             slot = group * UNROLL + at
-            col = jnp.where(slot < count, cols_ref[slot], col_blocks)
-            acc_ref[col] += jnp.dot(picked(slot), blocks_ref[slot], preferred_element_type=F32)
+            live = slot < count
+            col = jnp.where(live, cols_ref[0, slot], col_blocks)
+            picked = tokens_ref[:, pl.ds(pl.multiple_of(rows_ref[0, slot] * 128, 128), 128)]
+            picked_ref[slot] = picked * live.astype(BF16)
+            acc_ref[col] += jnp.dot(picked, blocks_ref[slot], preferred_element_type=F32)
         return carry
 
     lax.fori_loop(0, slots // UNROLL, forward, 0)
@@ -148,16 +156,12 @@
     def backward(group, carry):
         for at in range(UNROLL):
             slot = group * UNROLL + at
-            live = slot < count
-            row = jnp.where(live, rows_ref[slot], row_blocks)
-            grad = grad_pre_ref[cols_ref[slot]]
+            row = jnp.where(slot < count, rows_ref[0, slot], row_blocks)
+            grad = grad_pre_ref[cols_ref[0, slot]]
+            spread_ref[slot] = grad
             back_acc_ref[row] += lax.dot_general(
                 grad, blocks_ref[slot], (((1,), (1,)), ((), ())), preferred_element_type=F32
             )
-            partial = lax.dot_general(
-                picked(slot), grad, (((0,), (0,)), ((), ())), preferred_element_type=F32
-            )
-            grads_ref[slot] = (partial * live.astype(F32)).astype(BF16)
         return carry
 
     lax.fori_loop(0, slots // UNROLL, backward, 0)
@@ -169,8 +173,8 @@
 
 def local_work(rows, cols, count, tokens, blocks, cot, owners):
     tok, feat = tokens.shape
+    panel = cot.shape[1]
     slots = blocks.shape[0]
-    panel = cot.shape[1]
     smem = pl.BlockSpec(memory_space=pltpu.SMEM)
     vmem = pl.BlockSpec(memory_space=pltpu.VMEM)
     return pl.pallas_call(
@@ -178,10 +182,11 @@
         out_shape=(
             jax.ShapeDtypeStruct((tok, panel), BF16),
             jax.ShapeDtypeStruct((owners, tok, feat // owners), BF16),
-            jax.ShapeDtypeStruct((slots, 128, 128), BF16),
+            jax.ShapeDtypeStruct((slots, tok, 128), BF16),
+            jax.ShapeDtypeStruct((slots, tok, 128), BF16),
         ),
         in_specs=[smem, smem, smem, vmem, vmem, vmem],
-        out_specs=(vmem, vmem, vmem),
+        out_specs=(vmem, vmem, vmem, vmem),
         scratch_shapes=[
             pltpu.VMEM((panel // 128 + 1, tok, 128), F32),
             pltpu.VMEM((panel // 128, tok, 128), BF16),
@@ -193,8 +198,9 @@
 
 
 def reduce_kernel(
-    scale, back_ref, grads_ref, in_grad_ref, block_grad_ref,
-    z_buf, y_buf, y_out, c_buf, x_sum, x_buf, h_out, h_buf,
+    scale, picked_ref, spread_ref, back_ref,
+    in_grad_ref, block_grad_ref,
+    z_buf, z_own, y_buf, y_out, c_buf, x_sum, x_buf, h_out, h_buf,
     z_send, z_recv, y_send, y_recv, c_send, c_recv, x_send, x_recv, h_send, h_recv,
 ):
     dp, weight = lax.axis_index("dp"), lax.axis_index("weight")
@@ -205,7 +211,7 @@
     sibling = weight + 1 - 2 * core
     x_weight = [(side * 2 + h) * 2 + core for side in x_sides]
     h_weight = (x * 2 + 1 - h) * 2 + core
-    greet(
+    ready = greet(
         [(mod(j + delta, NY) * NZ + z, weight) for delta in range(1, NY)]
         + [(j * NZ + side, weight) for side in sides]
         + [(dp, sibling)]
@@ -228,12 +234,23 @@
         ahead = hops(delta, side) - step
         return mod(j + delta, NY) * NZ + mod(z + (ahead if side == 0 else -ahead), NZ)
 
+    def block_grad(slot):
+        return lax.dot_general(
+            picked_ref[slot], spread_ref[slot], (((0,), (0,)), ((), ())),
+            preferred_element_type=F32,
+        )
+
     def z_copy(side, delta, step):
-        src = grads_ref.at[z_slot(side, delta, 0)] if step == 0 else z_buf.at[side, delta, step - 1]
+        src = z_own.at[side, delta] if step == 0 else z_buf.at[side, delta, step - 1]
         return send(
             src, z_buf.at[side, delta, step], z_send.at[side, delta, step],
             z_recv.at[side, delta, step], (j * NZ + sides[side], weight),
         )
+
+    def z_prepare():
+        for delta in range(NY):
+            for side in range(2):
+                z_own[side, delta] = block_grad(z_slot(side, delta, 0)).astype(BF16)
 
     def z_step(step):
         for delta in range(NY):
@@ -241,10 +258,10 @@
                 if step >= hops(delta, side):
                     continue
                 if step > 0:
+                    own = block_grad(z_slot(side, delta, step))
                     z_copy(side, delta, step - 1).wait_recv()
                     z_buf[side, delta, step - 1] = (
-                        z_buf[side, delta, step - 1].astype(F32)
-                        + grads_ref[z_slot(side, delta, step)].astype(F32)
+                        z_buf[side, delta, step - 1].astype(F32) + own
                     ).astype(BF16)
                 go(z_copy(side, delta, step))
 
@@ -271,10 +288,10 @@
         return send(h_out, h_buf, h_send, h_recv, (dp, h_weight))
 
     order = [(2, 1), (2, 0), (3, 1), (1, 0), (1, 1), (3, 0), (0, 1), (0, 0)]
-    for dx, half in order[:2]:
-        go(c_copy(dx, half))
+    z_prepare()
+    ready()
     z_step(0)
-    for dx, half in order[2:]:
+    for dx, half in order:
         go(c_copy(dx, half))
     for half, side in ((1, 0), (0, 1)):
         x_sum[side, 0] = c_sum(2, half).astype(BF16)
@@ -305,7 +322,7 @@
     z_step(5)
 
     def z_total(delta):
-        value = grads_ref[mod(j + delta, NY) * NZ + z].astype(F32)
+        value = block_grad(mod(j + delta, NY) * NZ + z)
         for side in range(2):
             last = hops(delta, side) - 1
             z_copy(side, delta, last).wait_recv()
@@ -332,23 +349,24 @@
         copy.wait_send()
 
 
-def reduce_all(back, grads, scale):
+def reduce_all(picked, spread, back, scale):
     owners, tok, width = back.shape
     vmem = pl.BlockSpec(memory_space=pltpu.VMEM)
-    part = (tok, width)
+    part, block = (tok, width), (128, 128)
     dma = pltpu.SemaphoreType.DMA
     return pl.pallas_call(
         functools.partial(reduce_kernel, scale),
         out_shape=(
             jax.ShapeDtypeStruct(part, BF16),
-            jax.ShapeDtypeStruct(grads.shape[1:], F32),
+            jax.ShapeDtypeStruct(block, F32),
         ),
-        in_specs=[vmem, vmem],
+        in_specs=[vmem, vmem, vmem],
         out_specs=(vmem, vmem),
         scratch_shapes=[
-            pltpu.VMEM((2, NY, NZ // 2) + grads.shape[1:], BF16),
-            pltpu.VMEM((NY - 1,) + grads.shape[1:], BF16),
-            pltpu.VMEM((NY - 1,) + grads.shape[1:], BF16),
+            pltpu.VMEM((2, NY, NZ // 2) + block, BF16),
+            pltpu.VMEM((2, NY) + block, BF16),
+            pltpu.VMEM((NY - 1,) + block, BF16),
+            pltpu.VMEM((NY - 1,) + block, BF16),
             pltpu.VMEM((NX, 2) + part, BF16),
             pltpu.VMEM((2, 3) + part, BF16),
             pltpu.VMEM((2, 3) + part, BF16),
@@ -369,17 +387,18 @@
             collective_id=1, has_side_effects=True, vmem_limit_bytes=32 << 20
         ),
         name="reduce_all",
-    )(back, grads)
+    )(picked, spread, back)
 
 
 def local(tokens, block_values, block_rows, block_cols, block_counts, cotangent):
     owners = lax.axis_size("weight")
     blocks = gather_blocks(block_values[0, 0], block_rows.shape[1])
-    activated, back, grads = local_work(
-        block_rows[0], block_cols[0], block_counts, tokens, blocks, cotangent, owners
+    rows, cols, count = block_rows, block_cols, block_counts
+    activated, back, picked, spread = local_work(
+        rows, cols, count, tokens, blocks, cotangent, owners
     )
     scale = 1.0 / math.sqrt(tokens.shape[0] * lax.axis_size("dp"))
-    input_grad, block_grad = reduce_all(back, grads, scale)
+    input_grad, block_grad = reduce_all(picked, spread, back, scale)
     return (activated, input_grad, block_grad.reshape(block_values.shape))
 
 

time: 88.8 us -> 82.9 us (0.934)
  local copies, waits for them, and re-layouts: 6.63 us -> 2.05 us
  Pallas kernels: 80.1 us -> 79.1 us
    unnamed x12, local copies, waits for them, and re-layouts: 6.63 us -> 2.05 us
    pallas_call x1, Pallas kernels: 6.03 us -> 5.03 us  [local_work(): pl.pallas_call(local_kernel, out_shape=(jax.ShapeDtypeStruct((tok, panel)...]
where the time goes in v2:
time: 82.9 us; the launch traced here: 82.5 us
  Pallas kernels  79.1 us (95%)
  local copies, waits for them, and re-layouts  2.05 us (2%)
  between operations  1.34 us (2%)
    pallas_call x1, Pallas kernels, gather_blocks(): pl.pallas_call(gather_kernel, out_shape=jax.ShapeDtypeStruct((slots,) + s...  42 us
    pallas_call x1, Pallas kernels, reduce_all(): pl.pallas_call(functools.partial(reduce_kernel, scale), out_shape=(jax.Sh...  32.1 us
    pallas_call x1, Pallas kernels, local_work(): pl.pallas_call(local_kernel, out_shape=(jax.ShapeDtypeStruct((tok, panel)...  5.03 us
    unnamed x12, local copies, waits for them, and re-layouts  2.05 us

profile of v2, /device:TPU:6, one launch (start us, length us, event | category | flops | bytes accessed | tf_op | source)
XLA Modules:
  0.0 82.5 jit_solution(11250610016710156589)
XLA Ops:
  1.3 0.0 copy-start.4
  1.3 0.7 copy-done.4
  2.0 0.0 copy-start
  2.0 0.0 copy-start.1
  2.0 0.0 copy-start.2
  2.0 0.0 copy-start.3
  2.0 42.0 %gather_blocks.1.blocks_ref = bf16[48,128,128]{2,1,0:T(8,128)(2,1)S(1)} custom-call(bf16[128,128]{1,0:T(8,128)(2,1)S(1)} %bitcast.3), custom_call_target="tpu_custom_call" | custom-call | flops 40000000000 | bytes 60000000 | tf_op jit(solution)/shard_map/gather_blocks/pallas_call | solution.py:102
  44.0 0.0 copy-done
  44.0 0.0 copy-done.1
  44.0 0.0 copy-done.2
  44.1 0.0 copy-done.3
  44.1 5.0 %local_work.1 = (bf16[128,2048]{1,0:T(8,128)(2,1)}, bf16[16,128,512]{2,1,0:T(8,128)(2,1)S(1)}, bf16[48,128,128]{2,1,0:T(8,128)(2,1)S(1)}, bf16[48,128,128]{2,1,0:T(8,128)(2,1)S(1)}) custom-call(s32[1,48]{1,0:T(1,128)S(1)} %copy-done.2, s32[1,48]{1,0:T(1,128)S(1)} %copy-done.3, s32[1]{0:T(128)S(6)} %copy.11.count_ref, bf16[128,8192]{1,0:T(8,128)(2,1)S(1)} %copy-done, ...), custom_call_target="tpu_custom_call" | custom-call | tf_op jit(solution)/shard_map/local_work/pallas_call | solution.py:180
  49.1 32.1 %reduce_all.1 = (bf16[128,512]{1,0:T(8,128)(2,1)S(1)}, f32[128,128]{1,0:T(8,128)S(1)}) custom-call(bf16[48,128,128]{2,1,0:T(8,128)(2,1)S(1)} %get-tuple-element.10.picked_ref, bf16[48,128,128]{2,1,0:T(8,128)(2,1)S(1)} %get-tuple-element.11.spread_ref, bf16[16,128,512]{2,1,0:T(8,128)(2,1)S(1)} %get-tuple-element.12.back_ref), custom_call_target="tpu_custom_call" | custom-call | tf_op jit(solution)/shard_map/reduce_all/pallas_call | solution.py:357
  81.2 0.7 copy.12
  81.9 0.6 copy.13
Async XLA Ops:
  1.3 0.8 copy-start.4
  2.0 42.0 %copy-start = (bf16[128,8192]{1,0:T(8,128)(2,1)S(1)}, bf16[128,8192]{1,0:T(8,128)(2,1)}, u32[]{:S(2)}) copy-start(bf16[128,8192]{1,0:T(8,128)(2,1)} %tokens_ref.1) | copy-start | bytes 6291460
  2.0 42.0 %copy-start.1 = (bf16[128,2048]{1,0:T(8,128)(2,1)S(1)}, bf16[128,2048]{1,0:T(8,128)(2,1)}, u32[]{:S(2)}) copy-start(bf16[128,2048]{1,0:T(8,128)(2,1)} %cot_ref.1) | copy-start | bytes 1572868
  2.0 42.0 %copy-start.2 = (s32[1,48]{1,0:T(1,128)S(1)}, s32[1,48]{1,0:T(1,128)}, u32[]{:S(2)}) copy-start(s32[1,48]{1,0:T(1,128)} %rows_ref.1) | copy-start | bytes 580
  2.0 42.0 %copy-start.3 = (s32[1,48]{1,0:T(1,128)S(1)}, s32[1,48]{1,0:T(1,128)}, u32[]{:S(2)}) copy-start(s32[1,48]{1,0:T(1,128)} %cols_ref.1) | copy-start | bytes 580

commit v3 on v2

v3 whole, which is shorter than its diff:
```python
import functools
import math

import jax
import jax.numpy as jnp
from jax import lax
from jax.experimental import pallas as pl
from jax.experimental.pallas import tpu as pltpu
from jax.sharding import PartitionSpec as P

MESH = pl.DeviceIdType.MESH
NY, NZ, NX = 4, 12, 4
F32, BF16 = jnp.float32, jnp.bfloat16


GATHER_PARTS = 2
SUM_PARTS = 1


def rows_of(ref, part, parts):
    size = ref.shape[0] // parts
    return ref.at[pl.ds(part * size, size)]


def mod(a, n):
    return lax.rem(a + n, n)


def hops(delta, side):
    long_way, short_way = NZ // 2, NZ - 1 - NZ // 2
    return long_way if (delta + side) % 2 == 0 else short_way


def greet(partners):
    barrier = pltpu.get_barrier_semaphore()
    for dp, weight in partners:
        pl.semaphore_signal(barrier, inc=1, device_id=(dp, weight), device_id_type=MESH)

    def wait():
        pl.semaphore_wait(barrier, len(partners))

    return wait


def gather_kernel(own_ref, out_ref, own_sem, y_send, y_recv, z_send, z_recv):
    dp, weight = lax.axis_index("dp"), lax.axis_index("weight")
    j, z = dp // NZ, lax.rem(dp, NZ)
    sides = (mod(z + 1, NZ), mod(z - 1, NZ))
    ready = greet(
        [(mod(j + delta, NY) * NZ + z, weight) for delta in range(1, NY)]
        + [(j * NZ + side, weight) for side in sides]
    )
    keep = pltpu.make_async_copy(own_ref, out_ref.at[dp], own_sem)
    keep.start()
    ready()

    def send(src, dst, part, send_sem, recv_sem, device):
        return pltpu.make_async_remote_copy(
            src_ref=rows_of(src, part, GATHER_PARTS),
            dst_ref=rows_of(dst, part, GATHER_PARTS),
            send_sem=send_sem,
            recv_sem=recv_sem,
            device_id=(device, weight),
            device_id_type=MESH,
        )

    def y_copy(delta, part):
        at = (delta - 1, part)
        return send(
            own_ref, out_ref.at[dp], part, y_send.at[at], y_recv.at[at],
            mod(j + delta, NY) * NZ + z,
        )

    def z_copy(side, delta, step, part):
        back = -step if side == 0 else step
        slot = mod(j - delta, NY) * NZ + mod(z + back, NZ)
        src = own_ref if (delta == 0 and step == 0) else out_ref.at[slot]
        at = (side, delta, step, part)
        return send(
            src, out_ref.at[slot], part, z_send.at[at], z_recv.at[at], j * NZ + sides[side]
        )

    started = []

    def go(copy):
        copy.start()
        started.append(copy)

    def z_step(delta, step, part):
        for side in range(2):
            if step > hops(delta, side):
                continue
            if step > 0:
                z_copy(side, delta, step - 1, part).wait_recv()
            if step < hops(delta, side):
                go(z_copy(side, delta, step, part))

    for part in range(GATHER_PARTS):
        z_step(0, 0, part)
    for part in range(GATHER_PARTS):
        for delta in range(1, NY):
            go(y_copy(delta, part))
    for step in range(NZ // 2 + 1):
        for part in range(GATHER_PARTS):
            z_step(0, step + 1, part)
        for part in range(GATHER_PARTS):
            for delta in (1, 3, 2):
                if step == 0:
                    y_copy(delta, part).wait_recv()
                z_step(delta, step, part)
    for copy in started:
        copy.wait_send()
    keep.wait()


def gather_blocks(own, slots):
    size = own.shape
    vmem = pl.BlockSpec(memory_space=pltpu.VMEM)
    return pl.pallas_call(
        gather_kernel,
        out_shape=jax.ShapeDtypeStruct((slots,) + size, own.dtype),
        in_specs=[vmem],
        out_specs=vmem,
        scratch_shapes=[
            pltpu.SemaphoreType.DMA,
            pltpu.SemaphoreType.DMA((NY - 1, GATHER_PARTS)),
            pltpu.SemaphoreType.DMA((NY - 1, GATHER_PARTS)),
            pltpu.SemaphoreType.DMA((2, NY, NZ // 2, GATHER_PARTS)),
            pltpu.SemaphoreType.DMA((2, NY, NZ // 2, GATHER_PARTS)),
        ],
        compiler_params=pltpu.CompilerParams(
            collective_id=0, has_side_effects=True, vmem_limit_bytes=4 << 20
        ),
        cost_estimate=pl.CostEstimate(flops=40_000_000_000, bytes_accessed=60_000_000, transcendentals=0),
        name="gather_blocks",
    )(own)


UNROLL = 24


def local_kernel(
    rows_ref, cols_ref, count_ref, tokens_ref, blocks_ref, cot_ref,
    act_ref, picked_ref, spread_ref, before_ref, last_ref, acc_ref, grad_pre_ref,
):
    slots = blocks_ref.shape[0]
    col_blocks = grad_pre_ref.shape[0]
    count = count_ref[0]
    for row in range(last_ref.shape[0]):
        last_ref[row] = slots
    for slot in range(slots):
        row = rows_ref[0, slot]
        known = last_ref[row]
        before_ref[slot] = known
        last_ref[row] = jnp.where(slot < count, slot, known)
    acc_ref[...] = jnp.zeros_like(acc_ref)

    def forward(group, carry):
        for at in range(UNROLL):
            slot = group * UNROLL + at
            live = slot < count
            col = jnp.where(live, cols_ref[0, slot], col_blocks)
            picked = tokens_ref[:, pl.ds(pl.multiple_of(rows_ref[0, slot] * 128, 128), 128)]
            picked_ref[slot] = picked * live.astype(BF16)
            acc_ref[col] += jnp.dot(picked, blocks_ref[slot], preferred_element_type=F32)
        return carry

    lax.fori_loop(0, slots // UNROLL, forward, 0)
    for col in range(col_blocks):
        here = slice(col * 128, col * 128 + 128)
        preact = acc_ref[col]
        gate = jax.nn.sigmoid(preact)
        act_ref[:, here] = (preact * gate).astype(BF16)
        grad_pre_ref[col] = (
            cot_ref[:, here].astype(F32) * gate * (1.0 + preact * (1.0 - gate))
        ).astype(BF16)

    for slot in range(slots):
        spread_ref[slot] = grad_pre_ref[cols_ref[0, slot]]


def local_work(rows, cols, count, tokens, blocks, cot):
    tok, feat = tokens.shape
    panel = cot.shape[1]
    slots = blocks.shape[0]
    smem = pl.BlockSpec(memory_space=pltpu.SMEM)
    vmem = pl.BlockSpec(memory_space=pltpu.VMEM)
    return pl.pallas_call(
        local_kernel,
        out_shape=(
            jax.ShapeDtypeStruct((tok, panel), BF16),
            jax.ShapeDtypeStruct((slots, tok, 128), BF16),
            jax.ShapeDtypeStruct((slots, tok, 128), BF16),
            jax.ShapeDtypeStruct((slots,), jnp.int32),
            jax.ShapeDtypeStruct((feat // 128,), jnp.int32),
        ),
        in_specs=[smem, smem, smem, vmem, vmem, vmem],
        out_specs=(vmem, vmem, vmem, smem, smem),
        scratch_shapes=[
            pltpu.VMEM((panel // 128 + 1, tok, 128), F32),
            pltpu.VMEM((panel // 128, tok, 128), BF16),
        ],
        compiler_params=pltpu.CompilerParams(vmem_limit_bytes=32 << 20),
        name="local_work",
    )(rows, cols, count, tokens, blocks, cot)


def reduce_kernel(
    scale, before_ref, last_ref, picked_ref, spread_ref, blocks_ref, in_grad_ref, block_grad_ref,
    terms, back_ref, z_buf, z_own, z_first, y_buf, y_out, c_buf, x_sum, x_buf, h_out, h_buf,
    z_send, z_recv, y_send, y_recv, c_send, c_recv, x_send, x_recv, h_send, h_recv,
):
    dp, weight = lax.axis_index("dp"), lax.axis_index("weight")
    j, z = dp // NZ, lax.rem(dp, NZ)
    x, h, core = weight // 4, lax.rem(weight // 2, 2), lax.rem(weight, 2)
    sides = (mod(z + 1, NZ), mod(z - 1, NZ))
    x_sides = (mod(x + 1, NX), mod(x - 1, NX))
    sibling = weight + 1 - 2 * core
    x_weight = [(side * 2 + h) * 2 + core for side in x_sides]
    h_weight = (x * 2 + 1 - h) * 2 + core
    ready = greet(
        [(mod(j + delta, NY) * NZ + z, weight) for delta in range(1, NY)]
        + [(j * NZ + side, weight) for side in sides]
        + [(dp, sibling)]
        + [(dp, side) for side in x_weight]
        + [(dp, h_weight)]
    )
    started = []

    def go(copy):
        copy.start()
        started.append(copy)

    def send(src, dst, send_sem, recv_sem, device):
        return pltpu.make_async_remote_copy(
            src_ref=src, dst_ref=dst, send_sem=send_sem, recv_sem=recv_sem,
            device_id=device, device_id_type=MESH,
        )

    def z_slot(side, delta, step):
        ahead = hops(delta, side) - step
        return mod(j + delta, NY) * NZ + mod(z + (ahead if side == 0 else -ahead), NZ)

    def block_grad(slot):
        return lax.dot_general(
            picked_ref[slot], spread_ref[slot], (((0,), (0,)), ((), ())),
            preferred_element_type=F32,
        )

    def z_copy(side, delta, step, part):
        src = z_first.at[side, delta] if step == 0 else z_buf.at[side, delta, step - 1]
        at = (side, delta, step, part)
        return send(
            rows_of(src, part, SUM_PARTS), rows_of(z_buf.at[side, delta, step], part, SUM_PARTS),
            z_send.at[at], z_recv.at[at], (j * NZ + sides[side], weight),
        )

    def streams(step):
        return [(d, side) for d in range(NY) for side in range(2) if step < hops(d, side)]

    def z_prepare(step):
        for delta, side in streams(step):
            own = block_grad(z_slot(side, delta, step))
            if step == 0:
                z_first[side, delta] = own.astype(BF16)
            else:
                z_own[side, delta] = own

    def z_step(step):
        size = 128 // SUM_PARTS
        for part in range(SUM_PARTS):
            here = slice(part * size, part * size + size)
            for delta, side in streams(step):
                if step > 0:
                    z_copy(side, delta, step - 1, part).wait_recv()
                    z_buf[side, delta, step - 1, here] = (
                        z_buf[side, delta, step - 1, here].astype(F32) + z_own[side, delta, here]
                    ).astype(BF16)
                go(z_copy(side, delta, step, part))

    def back_terms():
        slots = blocks_ref.shape[0]
        terms[slots] = jnp.zeros_like(terms[slots])
        for slot in range(slots):
            terms[slot] = terms[before_ref[slot]] + lax.dot_general(
                spread_ref[slot], blocks_ref[slot], (((1,), (1,)), ((), ())),
                preferred_element_type=F32,
            )
        wide = back_ref.shape[2] // 128
        for row in range(last_ref.shape[0]):
            at = (row % wide) * 128
            back_ref[row // wide, :, at:at + 128] = terms[last_ref[row]].astype(BF16)

    def owner(dx, half, which):
        return (mod(x + dx, NX) * 2 + mod(h + half, 2)) * 2 + which

    def c_copy(dx, half):
        return send(
            back_ref.at[owner(dx, half, 1 - core)], c_buf.at[dx, half],
            c_send.at[dx, half], c_recv.at[dx, half], (dp, sibling),
        )

    def c_sum(dx, half):
        c_copy(dx, half).wait_recv()
        return c_buf[dx, half].astype(F32) + back_ref[owner(dx, half, core)].astype(F32)

    def x_copy(side, what, part=0, parts=1):
        at = (side, what, part)
        return send(
            rows_of(x_sum.at[side, what], part, parts), rows_of(x_buf.at[side, what], part, parts),
            x_send.at[at], x_recv.at[at], (dp, x_weight[side]),
        )

    def h_copy(part):
        return send(
            rows_of(h_out, part, 2), rows_of(h_buf, part, 2), h_send.at[part], h_recv.at[part],
            (dp, h_weight),
        )

    half_rows = h_out.shape[0] // 2
    halves = [(part, slice(part * half_rows, part * half_rows + half_rows)) for part in range(2)]

    z_prepare(0)
    ready()
    z_step(0)
    z_prepare(1)
    back_terms()
    for dx, half in [(2, 1), (2, 0), (1, 1), (3, 0), (1, 0), (3, 1), (0, 1), (0, 0)]:
        go(c_copy(dx, half))
    z_step(1)
    z_prepare(2)
    x_sum[0, 0] = c_sum(2, 1).astype(BF16)
    for part in range(2):
        go(x_copy(0, 0, part, 2))
    x_sum[1, 0] = c_sum(2, 0).astype(BF16)
    go(x_copy(1, 0))
    z_step(2)
    z_prepare(3)
    own_right, own_left = c_sum(1, 1), c_sum(3, 0)
    z_step(3)
    z_prepare(4)
    for part, here in halves:
        x_copy(0, 0, part, 2).wait_recv()
        x_sum[0, 2, here] = (own_right[here] + x_buf[0, 0, here].astype(F32)).astype(BF16)
        go(x_copy(0, 2, part, 2))
    x_sum[1, 1] = c_sum(3, 1).astype(BF16)
    go(x_copy(1, 1))
    x_sum[0, 1] = c_sum(1, 0).astype(BF16)
    go(x_copy(0, 1))
    z_step(4)
    z_prepare(5)
    x_copy(1, 0).wait_recv()
    x_sum[1, 2] = (own_left + x_buf[1, 0].astype(F32)).astype(BF16)
    go(x_copy(1, 2))
    total = c_sum(0, 1)
    z_step(5)
    x_copy(1, 1).wait_recv()
    total += x_buf[1, 1].astype(F32)
    for part, here in halves:
        x_copy(0, 2, part, 2).wait_recv()
        h_out[here] = (total[here] + x_buf[0, 2, here].astype(F32)).astype(BF16)
        go(h_copy(part))
    kept = [block_grad(mod(j + delta, NY) * NZ + z) for delta in range(NY)]

    def z_total(delta):
        value = kept[delta]
        for side in range(2):
            last = hops(delta, side) - 1
            for part in range(SUM_PARTS):
                z_copy(side, delta, last, part).wait_recv()
            value += z_buf[side, delta, last].astype(F32)
        return value

    def y_copy(delta):
        return send(
            y_out.at[delta - 1], y_buf.at[delta - 1], y_send.at[delta - 1], y_recv.at[delta - 1],
            (mod(j + delta, NY) * NZ + z, weight),
        )

    for delta in (2, 1, 3):
        y_out[delta - 1] = z_total(delta).astype(BF16)
        go(y_copy(delta))
    grad = z_total(0)
    total = c_sum(0, 0)
    x_copy(0, 1).wait_recv()
    total += x_buf[0, 1].astype(F32)
    x_copy(1, 2).wait_recv()
    total += x_buf[1, 2].astype(F32)
    for delta in (1, 3, 2):
        y_copy(delta).wait_recv()
        grad += y_buf[delta - 1].astype(F32)
    block_grad_ref[...] = grad * scale
    for part, here in halves:
        h_copy(part).wait_recv()
        in_grad_ref[here] = (total[here] + h_buf[here].astype(F32)).astype(BF16)
    for copy in started:
        copy.wait_send()


def reduce_all(before, last, picked, spread, blocks, owners, scale):
    slots, tok = picked.shape[:2]
    vmem, smem = pl.BlockSpec(memory_space=pltpu.VMEM), pl.BlockSpec(memory_space=pltpu.SMEM)
    part, block = (tok, last.shape[0] * 128 // owners), (128, 128)
    dma = pltpu.SemaphoreType.DMA
    return pl.pallas_call(
        functools.partial(reduce_kernel, scale),
        out_shape=(
            jax.ShapeDtypeStruct(part, BF16),
            jax.ShapeDtypeStruct(block, F32),
        ),
        in_specs=[smem, smem, vmem, vmem, vmem],
        out_specs=(vmem, vmem),
        scratch_shapes=[
            pltpu.VMEM((slots + 1, tok, 128), F32),
            pltpu.VMEM((owners,) + part, BF16),
            pltpu.VMEM((2, NY, NZ // 2) + block, BF16),
            pltpu.VMEM((2, NY) + block, F32),
            pltpu.VMEM((2, NY) + block, BF16),
            pltpu.VMEM((NY - 1,) + block, BF16),
            pltpu.VMEM((NY - 1,) + block, BF16),
            pltpu.VMEM((NX, 2) + part, BF16),
            pltpu.VMEM((2, 3) + part, BF16),
            pltpu.VMEM((2, 3) + part, BF16),
            pltpu.VMEM(part, BF16),
            pltpu.VMEM(part, BF16),
            dma((2, NY, NZ // 2, SUM_PARTS)),
            dma((2, NY, NZ // 2, SUM_PARTS)),
            dma((NY - 1,)),
            dma((NY - 1,)),
            dma((NX, 2)),
            dma((NX, 2)),
            dma((2, 3, 2)),
            dma((2, 3, 2)),
            dma((2,)),
            dma((2,)),
        ],
        compiler_params=pltpu.CompilerParams(
            collective_id=1, has_side_effects=True, vmem_limit_bytes=32 << 20
        ),
        name="reduce_all",
    )(before, last, picked, spread, blocks)


def local(tokens, block_values, block_rows, block_cols, block_counts, cotangent):
    owners = lax.axis_size("weight")
    blocks = gather_blocks(block_values[0, 0], block_rows.shape[1])
    rows, cols, count = block_rows, block_cols, block_counts
    activated, picked, spread, before, last = local_work(
        rows, cols, count, tokens, blocks, cotangent
    )
    scale = 1.0 / math.sqrt(tokens.shape[0] * lax.axis_size("dp"))
    input_grad, block_grad = reduce_all(before, last, picked, spread, blocks, owners, scale)
    return (activated, input_grad, block_grad.reshape(block_values.shape))


def solution(mesh):
    placed = (
        P("dp", None),
        P("weight", "dp", None, None),
        P("weight", None),
        P("weight", None),
        P("weight"),
        P("dp", "weight"),
    )
    return jax.shard_map(
        local,
        mesh=mesh,
        in_specs=placed,
        out_specs=(P("dp", "weight"), P("dp", "weight"), P("weight", "dp", None, None)),
        check_vma=False,
    )
```

time: 82.9 us -> 81.4 us (0.982)
  Pallas kernels: 79.1 us -> 77.8 us
    pallas_call x1, Pallas kernels: 5.03 us -> 2.98 us  [local_work(): pl.pallas_call(local_kernel, out_shape=(jax.ShapeDtypeStruct((tok, panel)...]
where the time goes in v3:
time: 81.4 us; the launch traced here: 81.2 us
  Pallas kernels  77.8 us (96%)
  local copies, waits for them, and re-layouts  2.05 us (3%)
  between operations  1.35 us (2%)
    pallas_call x1, Pallas kernels, gather_blocks(): pl.pallas_call(gather_kernel, out_shape=jax.ShapeDtypeStruct((slots,) + s...  42.5 us
    pallas_call x1, Pallas kernels, reduce_all(): pl.pallas_call(functools.partial(reduce_kernel, scale), out_shape=(jax.Sh...  32.3 us
    pallas_call x1, Pallas kernels, local_work(): pl.pallas_call(local_kernel, out_shape=(jax.ShapeDtypeStruct((tok, panel)...  2.98 us
    unnamed x12, local copies, waits for them, and re-layouts  2.05 us

profile of v3, /device:TPU:6, one launch (start us, length us, event | category | flops | bytes accessed | tf_op | source)
XLA Modules:
  0.0 81.2 jit_solution(1021797726026412130)
XLA Ops:
  1.3 0.0 copy-start.4
  1.3 0.7 copy-done.4
  2.0 0.0 copy-start
  2.0 0.0 copy-start.1
  2.0 0.0 copy-start.2
  2.0 0.0 copy-start.3
  2.0 42.5 %gather_blocks.1.blocks_ref = bf16[48,128,128]{2,1,0:T(8,128)(2,1)S(1)} custom-call(bf16[128,128]{1,0:T(8,128)(2,1)S(1)} %bitcast.3), custom_call_target="tpu_custom_call" | custom-call | flops 40000000000 | bytes 60000000 | tf_op jit(solution)/shard_map/gather_blocks/pallas_call | solution.py:119
  44.6 0.0 copy-done
  44.6 0.0 copy-done.1
  44.6 0.0 copy-done.2
  44.6 0.0 copy-done.3
  44.6 3.0 %local_work.1 = (bf16[128,2048]{1,0:T(8,128)(2,1)}, bf16[48,128,128]{2,1,0:T(8,128)(2,1)S(1)}, bf16[48,128,128]{2,1,0:T(8,128)(2,1)S(1)}, s32[48]{0:T(128)S(1)}, s32[64]{0:T(128)S(1)}) custom-call(s32[1,48]{1,0:T(1,128)S(1)} %copy-done.2, s32[1,48]{1,0:T(1,128)S(1)} %copy-done.3, s32[1]{0:T(128)S(6)} %copy.11.count_ref, bf16[128,8192]{1,0:T(8,128)(2,1)S(1)} %copy-done, ...), custom_call_target="tpu_custom_call" | custom-call | tf_op jit(solution)/shard_map/local_work/pallas_call | solution.py:188
  47.6 32.3 %reduce_all.1 = (bf16[128,512]{1,0:T(8,128)(2,1)S(1)}, f32[128,128]{1,0:T(8,128)S(1)}) custom-call(s32[48]{0:T(128)S(1)} %get-tuple-element.11.before_ref, s32[64]{0:T(128)S(1)} %get-tuple-element.12.last_ref, bf16[48,128,128]{2,1,0:T(8,128)(2,1)S(1)} %get-tuple-element.13.picked_ref, bf16[48,128,128]{2,1,0:T(8,128)(2,1)S(1)} %get-tuple-element.14.spread_ref, ...), custom_call_target="tpu_custom_call" | custom-call | tf_op jit(solution)/shard_map/reduce_all/pallas_call | solution.py:405
  79.9 0.7 copy.12
  80.6 0.6 copy.13
Async XLA Ops:
  1.3 0.8 copy-start.4
  2.0 42.5 %copy-start = (bf16[128,8192]{1,0:T(8,128)(2,1)S(1)}, bf16[128,8192]{1,0:T(8,128)(2,1)}, u32[]{:S(2)}) copy-start(bf16[128,8192]{1,0:T(8,128)(2,1)} %tokens_ref.1) | copy-start | bytes 6291460
  2.0 42.5 %copy-start.1 = (bf16[128,2048]{1,0:T(8,128)(2,1)S(1)}, bf16[128,2048]{1,0:T(8,128)(2,1)}, u32[]{:S(2)}) copy-start(bf16[128,2048]{1,0:T(8,128)(2,1)} %cot_ref.1) | copy-start | bytes 1572868
  2.0 42.6 %copy-start.2 = (s32[1,48]{1,0:T(1,128)S(1)}, s32[1,48]{1,0:T(1,128)}, u32[]{:S(2)}) copy-start(s32[1,48]{1,0:T(1,128)} %rows_ref.1) | copy-start | bytes 580
  2.0 42.6 %copy-start.3 = (s32[1,48]{1,0:T(1,128)S(1)}, s32[1,48]{1,0:T(1,128)}, u32[]{:S(2)}) copy-start(s32[1,48]{1,0:T(1,128)} %cols_ref.1) | copy-start | bytes 580

commit v4 on v3

--- a/solution.py
+++ b/solution.py
@@ -13,8 +13,15 @@
 F32, BF16 = jnp.float32, jnp.bfloat16
 
 
-GATHER_PARTS = 2
-SUM_PARTS = 1
+Y_ROWS = 96
+
+
+def stripe(ref, delta):
+    return ref if delta == 0 else ref.at[pl.ds(0, Y_ROWS)]
+
+
+def rest(ref):
+    return ref.at[pl.ds(Y_ROWS, ref.shape[0] - Y_ROWS)]
 
 
 def rows_of(ref, part, parts):
@@ -29,6 +36,13 @@
 def hops(delta, side):
     long_way, short_way = NZ // 2, NZ - 1 - NZ // 2
     return long_way if (delta + side) % 2 == 0 else short_way
+
+
+LONG = NZ // 2
+
+
+def is_long(delta, side):
+    return hops(delta, side) == LONG
 
 
 def greet(partners):
@@ -42,42 +56,49 @@
     return wait
 
 
-def gather_kernel(own_ref, out_ref, own_sem, y_send, y_recv, z_send, z_recv):
+def gather_kernel(own_ref, out_ref, own_sem, y_send, y_recv, z_send, z_recv, r_send, r_recv):
     dp, weight = lax.axis_index("dp"), lax.axis_index("weight")
     j, z = dp // NZ, lax.rem(dp, NZ)
     sides = (mod(z + 1, NZ), mod(z - 1, NZ))
+    far = (mod(z + 2, NZ), mod(z - 2, NZ))
     ready = greet(
         [(mod(j + delta, NY) * NZ + z, weight) for delta in range(1, NY)]
-        + [(j * NZ + side, weight) for side in sides]
+        + [(j * NZ + side, weight) for side in sides + far]
     )
     keep = pltpu.make_async_copy(own_ref, out_ref.at[dp], own_sem)
     keep.start()
     ready()
 
-    def send(src, dst, part, send_sem, recv_sem, device):
+    def send(src, dst, send_sem, recv_sem, device):
         return pltpu.make_async_remote_copy(
-            src_ref=rows_of(src, part, GATHER_PARTS),
-            dst_ref=rows_of(dst, part, GATHER_PARTS),
-            send_sem=send_sem,
-            recv_sem=recv_sem,
-            device_id=(device, weight),
-            device_id_type=MESH,
-        )
-
-    def y_copy(delta, part):
-        at = (delta - 1, part)
-        return send(
-            own_ref, out_ref.at[dp], part, y_send.at[at], y_recv.at[at],
+            src_ref=src, dst_ref=dst, send_sem=send_sem, recv_sem=recv_sem,
+            device_id=(device, weight), device_id_type=MESH,
+        )
+
+    def y_copy(delta):
+        return send(
+            own_ref, out_ref.at[dp], y_send.at[delta - 1], y_recv.at[delta - 1],
             mod(j + delta, NY) * NZ + z,
         )
 
-    def z_copy(side, delta, step, part):
-        back = -step if side == 0 else step
+    def z_copy(side, delta, step):
+        held = min(step, LONG - 2)
+        back = -held if side == 0 else held
         slot = mod(j - delta, NY) * NZ + mod(z + back, NZ)
         src = own_ref if (delta == 0 and step == 0) else out_ref.at[slot]
-        at = (side, delta, step, part)
-        return send(
-            src, out_ref.at[slot], part, z_send.at[at], z_recv.at[at], j * NZ + sides[side]
+        at = (side, delta, step)
+        return send(
+            stripe(src, delta), stripe(out_ref.at[slot], delta), z_send.at[at], z_recv.at[at],
+            j * NZ + (far if step == LONG - 1 else sides)[side],
+        )
+
+    def rest_copy(delta, side, step):
+        back = -step - 1 if side == 0 else step + 1
+        slot = j * NZ + mod(z + back, NZ)
+        at = (delta - 1, side, step)
+        return send(
+            rest(out_ref.at[slot]), rest(out_ref.at[slot]), r_send.at[at], r_recv.at[at],
+            mod(j + delta, NY) * NZ + z,
         )
 
     started = []
@@ -86,28 +107,34 @@
         copy.start()
         started.append(copy)
 
-    def z_step(delta, step, part):
+    def z_step(delta, step):
         for side in range(2):
             if step > hops(delta, side):
                 continue
             if step > 0:
-                z_copy(side, delta, step - 1, part).wait_recv()
-            if step < hops(delta, side):
-                go(z_copy(side, delta, step, part))
-
-    for part in range(GATHER_PARTS):
-        z_step(0, 0, part)
-    for part in range(GATHER_PARTS):
-        for delta in range(1, NY):
-            go(y_copy(delta, part))
+                z_copy(side, delta, step - 1).wait_recv()
+            if step < min(hops(delta, side), LONG - 1):
+                go(z_copy(side, delta, step))
+            if step == LONG - 2 and is_long(delta, side):
+                go(z_copy(side, delta, LONG - 1))
+        for side in range(2):
+            if delta == 0 and 0 < step <= hops(0, side):
+                for other in range(1, NY):
+                    go(rest_copy(other, side, step - 1))
+
+    z_step(0, 0)
+    for delta in range(1, NY):
+        go(y_copy(delta))
     for step in range(NZ // 2 + 1):
-        for part in range(GATHER_PARTS):
-            z_step(0, step + 1, part)
-        for part in range(GATHER_PARTS):
-            for delta in (1, 3, 2):
-                if step == 0:
-                    y_copy(delta, part).wait_recv()
-                z_step(delta, step, part)
+        z_step(0, step + 1)
+        for delta in (1, 3, 2):
+            if step == 0:
+                y_copy(delta).wait_recv()
+            z_step(delta, step)
+    for side in range(2):
+        for step in range(hops(0, side)):
+            for delta in range(1, NY):
+                rest_copy(delta, side, step).wait_recv()
     for copy in started:
         copy.wait_send()
     keep.wait()
@@ -123,10 +150,12 @@
         out_specs=vmem,
         scratch_shapes=[
             pltpu.SemaphoreType.DMA,
-            pltpu.SemaphoreType.DMA((NY - 1, GATHER_PARTS)),
-            pltpu.SemaphoreType.DMA((NY - 1, GATHER_PARTS)),
-            pltpu.SemaphoreType.DMA((2, NY, NZ // 2, GATHER_PARTS)),
-            pltpu.SemaphoreType.DMA((2, NY, NZ // 2, GATHER_PARTS)),
+            pltpu.SemaphoreType.DMA((NY - 1,)),
+            pltpu.SemaphoreType.DMA((NY - 1,)),
+            pltpu.SemaphoreType.DMA((2, NY, NZ // 2)),
+            pltpu.SemaphoreType.DMA((2, NY, NZ // 2)),
+            pltpu.SemaphoreType.DMA((NY - 1, 2, NZ // 2)),
+            pltpu.SemaphoreType.DMA((NY - 1, 2, NZ // 2)),
         ],
         compiler_params=pltpu.CompilerParams(
             collective_id=0, has_side_effects=True, vmem_limit_bytes=4 << 20
@@ -207,20 +236,22 @@
 
 def reduce_kernel(
     scale, before_ref, last_ref, picked_ref, spread_ref, blocks_ref, in_grad_ref, block_grad_ref,
-    terms, back_ref, z_buf, z_own, z_first, y_buf, y_out, c_buf, x_sum, x_buf, h_out, h_buf,
-    z_send, z_recv, y_send, y_recv, c_send, c_recv, x_send, x_recv, h_send, h_recv,
+    terms, back_ref, z_buf, z_own, z_first, r_buf, r_out, y_buf, y_out, c_buf, x_sum, x_buf, h_out, h_buf,
+    z_send, z_recv, r_send, r_recv, y_send, y_recv, c_send, c_recv, x_send, x_recv,
+    h_send, h_recv,
 ):
     dp, weight = lax.axis_index("dp"), lax.axis_index("weight")
     j, z = dp // NZ, lax.rem(dp, NZ)
     x, h, core = weight // 4, lax.rem(weight // 2, 2), lax.rem(weight, 2)
     sides = (mod(z + 1, NZ), mod(z - 1, NZ))
+    far = (mod(z + 2, NZ), mod(z - 2, NZ))
     x_sides = (mod(x + 1, NX), mod(x - 1, NX))
     sibling = weight + 1 - 2 * core
     x_weight = [(side * 2 + h) * 2 + core for side in x_sides]
     h_weight = (x * 2 + 1 - h) * 2 + core
     ready = greet(
         [(mod(j + delta, NY) * NZ + z, weight) for delta in range(1, NY)]
-        + [(j * NZ + side, weight) for side in sides]
+        + [(j * NZ + side, weight) for side in sides + far]
         + [(dp, sibling)]
         + [(dp, side) for side in x_weight]
         + [(dp, h_weight)]
@@ -237,46 +268,67 @@
             device_id=device, device_id_type=MESH,
         )
 
-    def z_slot(side, delta, step):
+    def offset(side, delta, step):
         ahead = hops(delta, side) - step
-        return mod(j + delta, NY) * NZ + mod(z + (ahead if side == 0 else -ahead), NZ)
-
-    def block_grad(slot):
-        return lax.dot_general(
+        return ahead if side == 0 else NZ - ahead
+
+    def block_grad(delta, off):
+        slot = mod(j + delta, NY) * NZ + mod(z + off, NZ)
+        z_own[delta, off] = lax.dot_general(
             picked_ref[slot], spread_ref[slot], (((0,), (0,)), ((), ())),
             preferred_element_type=F32,
         )
-
-    def z_copy(side, delta, step, part):
-        src = z_first.at[side, delta] if step == 0 else z_buf.at[side, delta, step - 1]
-        at = (side, delta, step, part)
-        return send(
-            rows_of(src, part, SUM_PARTS), rows_of(z_buf.at[side, delta, step], part, SUM_PARTS),
-            z_send.at[at], z_recv.at[at], (j * NZ + sides[side], weight),
-        )
-
-    def streams(step):
-        return [(d, side) for d in range(NY) for side in range(2) if step < hops(d, side)]
-
-    def z_prepare(step):
-        for delta, side in streams(step):
-            own = block_grad(z_slot(side, delta, step))
-            if step == 0:
-                z_first[side, delta] = own.astype(BF16)
-            else:
-                z_own[side, delta] = own
-
-    def z_step(step):
-        size = 128 // SUM_PARTS
-        for part in range(SUM_PARTS):
-            here = slice(part * size, part * size + size)
-            for delta, side in streams(step):
-                if step > 0:
-                    z_copy(side, delta, step - 1, part).wait_recv()
-                    z_buf[side, delta, step - 1, here] = (
-                        z_buf[side, delta, step - 1, here].astype(F32) + z_own[side, delta, here]
-                    ).astype(BF16)
-                go(z_copy(side, delta, step, part))
+        if delta > 0 and off > 0:
+            r_out[delta - 1, off] = z_own[delta, off, Y_ROWS:].astype(BF16)
+
+    def rest_copy(delta, off):
+        at = (delta - 1, off)
+        return send(
+            r_out.at[at], r_buf.at[at], r_send.at[at], r_recv.at[at],
+            (mod(j + delta, NY) * NZ + z, weight),
+        )
+
+    def z_copy(side, delta, step):
+        if step == 0 or (step == 1 and is_long(delta, side)):
+            src = z_first.at[side, delta, step]
+        else:
+            src = z_buf.at[side, delta, step - 1]
+        at = (side, delta, step)
+        target = far if step == 0 and is_long(delta, side) else sides
+        return send(
+            stripe(src, delta), stripe(z_buf.at[at], delta), z_send.at[at], z_recv.at[at],
+            (j * NZ + target[side], weight),
+        )
+
+    def z_add(side, delta, step):
+        off = offset(side, delta, step)
+        if delta == 0:
+            for other in range(1, NY):
+                rest_copy(other, off).wait_recv()
+                z_own[0, off, Y_ROWS:] += r_buf[other - 1, off].astype(F32)
+        many = 128 if delta == 0 else Y_ROWS
+        own = z_own[delta, off, :many]
+        if step == 0 or (step == 1 and is_long(delta, side)):
+            z_first[side, delta, step, :many] = own.astype(BF16)
+        else:
+            if step == 2 and is_long(delta, side):
+                z_copy(side, delta, 0).wait_recv()
+                own += z_buf[side, delta, 0, :many].astype(F32)
+            z_copy(side, delta, step - 1).wait_recv()
+            z_buf[side, delta, step - 1, :many] = (
+                z_buf[side, delta, step - 1, :many].astype(F32) + own
+            ).astype(BF16)
+        go(z_copy(side, delta, step))
+
+    def z_step(turn, deltas):
+        for delta in deltas:
+            for side in range(2):
+                if turn == 0:
+                    z_add(side, delta, 0)
+                if is_long(delta, side):
+                    z_add(side, delta, turn + 1)
+                elif turn > 0:
+                    z_add(side, delta, turn)
 
     def back_terms():
         slots = blocks_ref.shape[0]
@@ -320,56 +372,67 @@
     half_rows = h_out.shape[0] // 2
     halves = [(part, slice(part * half_rows, part * half_rows + half_rows)) for part in range(2)]
 
-    z_prepare(0)
+    others, own = (2, 1, 3), (0,)
+    middle = NZ // 2
+    offs = sorted(range(NZ), key=lambda off: (abs(off - middle), off > middle))
+    first = offs[:3]
+    for off in first:
+        for delta in range(NY):
+            block_grad(delta, off)
     ready()
-    z_step(0)
-    z_prepare(1)
+    for off in first:
+        for delta in range(1, NY):
+            go(rest_copy(delta, off))
+    z_step(0, others)
+    for off in offs[3:]:
+        for delta in range(NY):
+            block_grad(delta, off)
+        if off > 0:
+            for delta in range(1, NY):
+                go(rest_copy(delta, off))
     back_terms()
     for dx, half in [(2, 1), (2, 0), (1, 1), (3, 0), (1, 0), (3, 1), (0, 1), (0, 0)]:
         go(c_copy(dx, half))
-    z_step(1)
-    z_prepare(2)
+    z_step(1, others)
+    z_step(0, own)
     x_sum[0, 0] = c_sum(2, 1).astype(BF16)
     for part in range(2):
         go(x_copy(0, 0, part, 2))
     x_sum[1, 0] = c_sum(2, 0).astype(BF16)
     go(x_copy(1, 0))
-    z_step(2)
-    z_prepare(3)
+    z_step(2, others)
+    z_step(1, own)
     own_right, own_left = c_sum(1, 1), c_sum(3, 0)
-    z_step(3)
-    z_prepare(4)
     for part, here in halves:
         x_copy(0, 0, part, 2).wait_recv()
         x_sum[0, 2, here] = (own_right[here] + x_buf[0, 0, here].astype(F32)).astype(BF16)
         go(x_copy(0, 2, part, 2))
+    z_step(3, others)
+    z_step(2, own)
     x_sum[1, 1] = c_sum(3, 1).astype(BF16)
     go(x_copy(1, 1))
     x_sum[0, 1] = c_sum(1, 0).astype(BF16)
     go(x_copy(0, 1))
-    z_step(4)
-    z_prepare(5)
     x_copy(1, 0).wait_recv()
     x_sum[1, 2] = (own_left + x_buf[1, 0].astype(F32)).astype(BF16)
     go(x_copy(1, 2))
     total = c_sum(0, 1)
-    z_step(5)
+    z_step(4, others)
+    z_step(3, own)
     x_copy(1, 1).wait_recv()
     total += x_buf[1, 1].astype(F32)
     for part, here in halves:
         x_copy(0, 2, part, 2).wait_recv()
         h_out[here] = (total[here] + x_buf[0, 2, here].astype(F32)).astype(BF16)
         go(h_copy(part))
-    kept = [block_grad(mod(j + delta, NY) * NZ + z) for delta in range(NY)]
 
     def z_total(delta):
-        value = kept[delta]
+        many = 128 if delta == 0 else Y_ROWS
         for side in range(2):
             last = hops(delta, side) - 1
-            for part in range(SUM_PARTS):
-                z_copy(side, delta, last, part).wait_recv()
-            value += z_buf[side, delta, last].astype(F32)
-        return value
+            z_copy(side, delta, last).wait_recv()
+            z_own[delta, 0, :many] += z_buf[side, delta, last, :many].astype(F32)
+        return z_own[delta, 0]
 
     def y_copy(delta):
         return send(
@@ -377,9 +440,10 @@
             (mod(j + delta, NY) * NZ + z, weight),
         )
 
-    for delta in (2, 1, 3):
+    for delta in others:
         y_out[delta - 1] = z_total(delta).astype(BF16)
         go(y_copy(delta))
+    z_step(4, own)
     grad = z_total(0)
     total = c_sum(0, 0)
     x_copy(0, 1).wait_recv()
@@ -414,8 +478,10 @@
             pltpu.VMEM((slots + 1, tok, 128), F32),
             pltpu.VMEM((owners,) + part, BF16),
             pltpu.VMEM((2, NY, NZ // 2) + block, BF16),
-            pltpu.VMEM((2, NY) + block, F32),
-            pltpu.VMEM((2, NY) + block, BF16),
+            pltpu.VMEM((NY, NZ) + block, F32),
+            pltpu.VMEM((2, NY, 2) + block, BF16),
+            pltpu.VMEM((NY - 1, NZ, 128 - Y_ROWS, 128), BF16),
+            pltpu.VMEM((NY - 1, NZ, 128 - Y_ROWS, 128), BF16),
             pltpu.VMEM((NY - 1,) + block, BF16),
             pltpu.VMEM((NY - 1,) + block, BF16),
             pltpu.VMEM((NX, 2) + part, BF16),
@@ -423,8 +489,10 @@
             pltpu.VMEM((2, 3) + part, BF16),
             pltpu.VMEM(part, BF16),
             pltpu.VMEM(part, BF16),
-            dma((2, NY, NZ // 2, SUM_PARTS)),
-            dma((2, NY, NZ // 2, SUM_PARTS)),
+            dma((2, NY, NZ // 2)),
+            dma((2, NY, NZ // 2)),
+            dma((NY - 1, NZ)),
+            dma((NY - 1, NZ)),
             dma((NY - 1,)),
             dma((NY - 1,)),
             dma((NX, 2)),

time: 81.4 us -> 80 us (0.983)
  the two profiles are of different devices: /device:TPU:6 before, /device:TPU:1 now
where the time goes in v4:
time: 80 us; the launch traced here: 79.8 us
  Pallas kernels  76.4 us (96%)
  local copies, waits for them, and re-layouts  2.05 us (3%)
  between operations  1.35 us (2%)
    pallas_call x1, Pallas kernels, reduce_all(): pl.pallas_call(functools.partial(reduce_kernel, scale), out_shape=(jax.Sh...  37.2 us
    pallas_call x1, Pallas kernels, gather_blocks(): pl.pallas_call(gather_kernel, out_shape=jax.ShapeDtypeStruct((slots,) + s...  36.2 us
    pallas_call x1, Pallas kernels, local_work(): pl.pallas_call(local_kernel, out_shape=(jax.ShapeDtypeStruct((tok, panel)...  2.97 us
    unnamed x12, local copies, waits for them, and re-layouts  2.05 us

profile of v4, /device:TPU:1, one launch (start us, length us, event | category | flops | bytes accessed | tf_op | source)
XLA Modules:
  0.0 79.8 jit_solution(3755880941672906299)
XLA Ops:
  1.3 0.0 copy-start.4
  1.3 0.7 copy-done.4
  2.0 0.0 copy-start
  2.0 0.0 copy-start.1
  2.0 0.0 copy-start.2
  2.0 0.0 copy-start.3
  2.0 36.2 %gather_blocks.1.blocks_ref = bf16[48,128,128]{2,1,0:T(8,128)(2,1)S(1)} custom-call(bf16[128,128]{1,0:T(8,128)(2,1)S(1)} %bitcast.3), custom_call_target="tpu_custom_call" | custom-call | flops 40000000000 | bytes 60000000 | tf_op jit(solution)/shard_map/gather_blocks/pallas_call | solution.py:146
  38.3 0.0 copy-done
  38.3 0.0 copy-done.1
  38.3 0.0 copy-done.2
  38.3 0.0 copy-done.3
  38.3 3.0 %local_work.1 = (bf16[128,2048]{1,0:T(8,128)(2,1)}, bf16[48,128,128]{2,1,0:T(8,128)(2,1)S(1)}, bf16[48,128,128]{2,1,0:T(8,128)(2,1)S(1)}, s32[48]{0:T(128)S(1)}, s32[64]{0:T(128)S(1)}) custom-call(s32[1,48]{1,0:T(1,128)S(1)} %copy-done.2, s32[1,48]{1,0:T(1,128)S(1)} %copy-done.3, s32[1]{0:T(128)S(6)} %copy.11.count_ref, bf16[128,8192]{1,0:T(8,128)(2,1)S(1)} %copy-done, ...), custom_call_target="tpu_custom_call" | custom-call | tf_op jit(solution)/shard_map/local_work/pallas_call | solution.py:217
  41.3 37.2 %reduce_all.1 = (bf16[128,512]{1,0:T(8,128)(2,1)S(1)}, f32[128,128]{1,0:T(8,128)S(1)}) custom-call(s32[48]{0:T(128)S(1)} %get-tuple-element.11.before_ref, s32[64]{0:T(128)S(1)} %get-tuple-element.12.last_ref, bf16[48,128,128]{2,1,0:T(8,128)(2,1)S(1)} %get-tuple-element.13.picked_ref, bf16[48,128,128]{2,1,0:T(8,128)(2,1)S(1)} %get-tuple-element.14.spread_ref, ...), custom_call_target="tpu_custom_call" | custom-call | tf_op jit(solution)/shard_map/reduce_all/pallas_call | solution.py:469
  78.5 0.7 copy.12
  79.2 0.6 copy.13
Async XLA Ops:
  1.3 0.8 copy-start.4
  2.0 36.2 %copy-start = (bf16[128,8192]{1,0:T(8,128)(2,1)S(1)}, bf16[128,8192]{1,0:T(8,128)(2,1)}, u32[]{:S(2)}) copy-start(bf16[128,8192]{1,0:T(8,128)(2,1)} %tokens_ref.1) | copy-start | bytes 6291460
  2.0 36.2 %copy-start.1 = (bf16[128,2048]{1,0:T(8,128)(2,1)S(1)}, bf16[128,2048]{1,0:T(8,128)(2,1)}, u32[]{:S(2)}) copy-start(bf16[128,2048]{1,0:T(8,128)(2,1)} %cot_ref.1) | copy-start | bytes 1572868
  2.0 36.2 %copy-start.2 = (s32[1,48]{1,0:T(1,128)S(1)}, s32[1,48]{1,0:T(1,128)}, u32[]{:S(2)}) copy-start(s32[1,48]{1,0:T(1,128)} %rows_ref.1) | copy-start | bytes 580
  2.0 36.2 %copy-start.3 = (s32[1,48]{1,0:T(1,128)S(1)}, s32[1,48]{1,0:T(1,128)}, u32[]{:S(2)}) copy-start(s32[1,48]{1,0:T(1,128)} %cols_ref.1) | copy-start | bytes 580

commit v5 on v4

--- a/solution.py
+++ b/solution.py
@@ -384,47 +384,47 @@
         for delta in range(1, NY):
             go(rest_copy(delta, off))
     z_step(0, others)
+    back_terms()
+    for dx, half in [(2, 1), (3, 1), (2, 0), (1, 1), (3, 0), (1, 0), (0, 1), (0, 0)]:
+        go(c_copy(dx, half))
     for off in offs[3:]:
         for delta in range(NY):
             block_grad(delta, off)
         if off > 0:
             for delta in range(1, NY):
                 go(rest_copy(delta, off))
-    back_terms()
-    for dx, half in [(2, 1), (2, 0), (1, 1), (3, 0), (1, 0), (3, 1), (0, 1), (0, 0)]:
-        go(c_copy(dx, half))
-    z_step(1, others)
-    z_step(0, own)
     x_sum[0, 0] = c_sum(2, 1).astype(BF16)
     for part in range(2):
         go(x_copy(0, 0, part, 2))
+    z_step(1, others)
+    x_sum[1, 1] = c_sum(3, 1).astype(BF16)
+    go(x_copy(1, 1))
+    z_step(0, own)
     x_sum[1, 0] = c_sum(2, 0).astype(BF16)
     go(x_copy(1, 0))
+    own_right, own_left = c_sum(1, 1), c_sum(3, 0)
     z_step(2, others)
     z_step(1, own)
-    own_right, own_left = c_sum(1, 1), c_sum(3, 0)
     for part, here in halves:
         x_copy(0, 0, part, 2).wait_recv()
         x_sum[0, 2, here] = (own_right[here] + x_buf[0, 0, here].astype(F32)).astype(BF16)
         go(x_copy(0, 2, part, 2))
+    x_sum[0, 1] = c_sum(1, 0).astype(BF16)
+    go(x_copy(0, 1))
+    total = c_sum(0, 1)
     z_step(3, others)
     z_step(2, own)
-    x_sum[1, 1] = c_sum(3, 1).astype(BF16)
-    go(x_copy(1, 1))
-    x_sum[0, 1] = c_sum(1, 0).astype(BF16)
-    go(x_copy(0, 1))
     x_copy(1, 0).wait_recv()
     x_sum[1, 2] = (own_left + x_buf[1, 0].astype(F32)).astype(BF16)
     go(x_copy(1, 2))
-    total = c_sum(0, 1)
-    z_step(4, others)
-    z_step(3, own)
     x_copy(1, 1).wait_recv()
     total += x_buf[1, 1].astype(F32)
     for part, here in halves:
         x_copy(0, 2, part, 2).wait_recv()
         h_out[here] = (total[here] + x_buf[0, 2, here].astype(F32)).astype(BF16)
         go(h_copy(part))
+    z_step(4, others)
+    z_step(3, own)
 
     def z_total(delta):
         many = 128 if delta == 0 else Y_ROWS

time: 80 us -> 77 us (0.963)
  the two profiles are of different devices: /device:TPU:1 before, /device:TPU:6 now
where the time goes in v5:
time: 77 us; the launch traced here: 76.8 us
  Pallas kernels  73.4 us (95%)
  local copies, waits for them, and re-layouts  2.05 us (3%)
  between operations  1.35 us (2%)
    pallas_call x1, Pallas kernels, gather_blocks(): pl.pallas_call(gather_kernel, out_shape=jax.ShapeDtypeStruct((slots,) + s...  39.4 us
    pallas_call x1, Pallas kernels, reduce_all(): pl.pallas_call(functools.partial(reduce_kernel, scale), out_shape=(jax.Sh...  31 us
    pallas_call x1, Pallas kernels, local_work(): pl.pallas_call(local_kernel, out_shape=(jax.ShapeDtypeStruct((tok, panel)...  2.98 us
    unnamed x12, local copies, waits for them, and re-layouts  2.05 us

profile of v5, /device:TPU:6, one launch (start us, length us, event | category | flops | bytes accessed | tf_op | source)
XLA Modules:
  0.0 76.8 jit_solution(4157691688026180908)
XLA Ops:
  1.3 0.0 copy-start.4
  1.3 0.7 copy-done.4
  2.0 0.0 copy-start
  2.0 0.0 copy-start.1
  2.0 0.0 copy-start.2
  2.0 0.0 copy-start.3
  2.0 39.4 %gather_blocks.1.blocks_ref = bf16[48,128,128]{2,1,0:T(8,128)(2,1)S(1)} custom-call(bf16[128,128]{1,0:T(8,128)(2,1)S(1)} %bitcast.3), custom_call_target="tpu_custom_call" | custom-call | flops 40000000000 | bytes 60000000 | tf_op jit(solution)/shard_map/gather_blocks/pallas_call | solution.py:146
  41.5 0.0 copy-done
  41.5 0.0 copy-done.1
  41.5 0.0 copy-done.2
  41.5 0.0 copy-done.3
  41.5 3.0 %local_work.1 = (bf16[128,2048]{1,0:T(8,128)(2,1)}, bf16[48,128,128]{2,1,0:T(8,128)(2,1)S(1)}, bf16[48,128,128]{2,1,0:T(8,128)(2,1)S(1)}, s32[48]{0:T(128)S(1)}, s32[64]{0:T(128)S(1)}) custom-call(s32[1,48]{1,0:T(1,128)S(1)} %copy-done.2, s32[1,48]{1,0:T(1,128)S(1)} %copy-done.3, s32[1]{0:T(128)S(6)} %copy.11.count_ref, bf16[128,8192]{1,0:T(8,128)(2,1)S(1)} %copy-done, ...), custom_call_target="tpu_custom_call" | custom-call | tf_op jit(solution)/shard_map/local_work/pallas_call | solution.py:217
  44.5 31.0 %reduce_all.1 = (bf16[128,512]{1,0:T(8,128)(2,1)S(1)}, f32[128,128]{1,0:T(8,128)S(1)}) custom-call(s32[48]{0:T(128)S(1)} %get-tuple-element.11.before_ref, s32[64]{0:T(128)S(1)} %get-tuple-element.12.last_ref, bf16[48,128,128]{2,1,0:T(8,128)(2,1)S(1)} %get-tuple-element.13.picked_ref, bf16[48,128,128]{2,1,0:T(8,128)(2,1)S(1)} %get-tuple-element.14.spread_ref, ...), custom_call_target="tpu_custom_call" | custom-call | tf_op jit(solution)/shard_map/reduce_all/pallas_call | solution.py:469
  75.5 0.7 copy.12
  76.1 0.6 copy.13
Async XLA Ops:
  1.3 0.8 copy-start.4
  2.0 39.4 %copy-start = (bf16[128,8192]{1,0:T(8,128)(2,1)S(1)}, bf16[128,8192]{1,0:T(8,128)(2,1)}, u32[]{:S(2)}) copy-start(bf16[128,8192]{1,0:T(8,128)(2,1)} %tokens_ref.1) | copy-start | bytes 6291460
  2.0 39.5 %copy-start.1 = (bf16[128,2048]{1,0:T(8,128)(2,1)S(1)}, bf16[128,2048]{1,0:T(8,128)(2,1)}, u32[]{:S(2)}) copy-start(bf16[128,2048]{1,0:T(8,128)(2,1)} %cot_ref.1) | copy-start | bytes 1572868
  2.0 39.5 %copy-start.2 = (s32[1,48]{1,0:T(1,128)S(1)}, s32[1,48]{1,0:T(1,128)}, u32[]{:S(2)}) copy-start(s32[1,48]{1,0:T(1,128)} %rows_ref.1) | copy-start | bytes 580
  2.0 39.5 %copy-start.3 = (s32[1,48]{1,0:T(1,128)S(1)}, s32[1,48]{1,0:T(1,128)}, u32[]{:S(2)}) copy-start(s32[1,48]{1,0:T(1,128)} %cols_ref.1) | copy-start | bytes 580
